TPU v7x, 32 devices: a whole 2x2x4 slice. The times are simulated.
32 devices in a mesh: fsdp: 32 (over z, y, x, core).
Axes of the slice: x: 2, y: 2, z: 4, core: 2. Of those that a mesh axis runs over, the one named last changes fastest.
Arguments:
- tokens: bfloat16 [4096, 768], P('fsdp'), may hold values from -6 to 6
- attn_weight: bfloat16 [768, 3072], P(None, 'fsdp')
- w_gate: bfloat16 [768, 3072], P(None, 'fsdp'), may hold values from -0.21875 to 0.21875
- w_up: bfloat16 [768, 3072], P(None, 'fsdp'), may hold values from -0.21875 to 0.21875
- w_down: bfloat16 [3072, 768], P('fsdp'), may hold values from -0.109375 to 0.109375
- norm_gains: float32 [2, 768], replicated, may hold values from 0.5 to 1.5
- bias_table: float32 [32, 12], replicated, may hold values from -4 to 4
- router: float32 [768, 64], replicated, may hold values from -0.4375 to 0.4375
- grad_out: bfloat16 [4096, 768], P('fsdp'), may hold values from -6 to 6
- segment: int32 [4096], P('fsdp'), may hold values from -1 to 7, as said below
- expert_ids: int32 [4096, 2], P('fsdp'), may hold values from 0 to 63, as said below
- bucket_of: int32 [64], replicated, may hold values from 0 to 31, as said below
Outputs:
- result: bfloat16 [4096, 768], P('fsdp')
- grad_tokens: bfloat16 [4096, 768], P('fsdp')
- grad_attn: float32 [768, 3072], P(None, 'fsdp')
- grad_gate: float32 [768, 3072], P(None, 'fsdp')
- grad_up: float32 [768, 3072], P(None, 'fsdp')
- grad_down: float32 [3072, 768], P('fsdp')
- grad_gains: float32 [2, 768], replicated
- grad_table: float32 [32, 12], replicated
- grad_router: float32 [768, 64], replicated
Inputs may be any that keep to these rules, and one draw needn't show every extreme that they name: `segment`: each block of 64 slots is one micro-batch of one device; sequences take consecutive slots and are numbered 0 to 7 in order within a block; unused slots, marked -1, come at a block's end; the first block has no unused slot and reaches number 7. `expert_ids`: the two experts of a row differ. `bucket_of`: never falls as the distance grows; equal to the distance below 16.
All inputs are finite; a program needn't handle non-finite values.
Results may differ from a plain program's by a relative error of at most 0.012.
The roundings to bfloat16 on the way count: a program that leaves them out, or rounds other values in their place, can miss the bound.
Values may be sent and summed in bfloat16 or wider, within the bound.
A program may use at most 192 MiB of HBM per device.

v0:
```python
import jax
import jax.numpy as jnp
from jax import lax
from jax.sharding import PartitionSpec as P

EPSILON = 1e-06
HIGHEST = lax.Precision.HIGHEST


def gelu_tanh(inner):
    return jax.nn.gelu(inner, approximate=True)


def norm_back(inputs, scale, gain, upstream):
    weighted = gain * upstream
    return scale * weighted - inputs * scale * scale * scale * jnp.mean(
        weighted * inputs, axis=-1, keepdims=True
    )


def masked_scores(query, keyset, offsets, allowed, factor):
    raw = jnp.einsum("ihd,jhd->hij", query, keyset, preferred_element_type=jnp.float32)
    return jnp.where(allowed[None], raw * factor + offsets, -1e30)


def body(
    tokens,
    attn_weight,
    w_gate,
    w_up,
    w_down,
    norm_gains,
    bias_table,
    router,
    grad_out,
    segment,
    expert_ids,
    bucket_of,
):
    model_width = tokens.shape[1]
    slot_count = bucket_of.shape[0]
    micro_count = tokens.shape[0] // slot_count
    routed_count = router.shape[1]
    head_count = bias_table.shape[1]
    head_width = model_width // head_count
    factor = head_width ** (-0.5)
    triple_width = 3 * model_width
    places = jnp.arange(slot_count)
    distance = jnp.maximum(places[:, None] - places[None, :], 0)
    bucket_hit = (
        bucket_of[distance][:, :, None] == jnp.arange(bias_table.shape[0])[None, None, :]
    ).astype(jnp.float32)
    offsets = jnp.einsum("ijb,bh->hij", bucket_hit, bias_table, precision=HIGHEST)
    causal = places[None, :] <= places[:, None]
    first_hot = jnp.where(jnp.arange(routed_count) == 0, 1.0, 0.0)
    contract_rows = (((0,), (0,)), ((), ()))
    contract_cols = (((1,), (1,)), ((), ()))
    expert_shard = (
        jnp.zeros(w_gate.shape, jnp.float32),
        jnp.zeros(w_up.shape, jnp.float32),
        jnp.zeros(w_down.shape, jnp.float32),
    )
    local_sums = None
    grad_gains = jnp.zeros(norm_gains.shape, jnp.float32)
    grad_table = jnp.zeros(bias_table.shape, jnp.float32)
    grad_router = jnp.zeros(router.shape, jnp.float32)
    results = []
    input_grads = []
    for micro_step in range(micro_count):
        first_row = micro_step * slot_count
        inputs = tokens[first_row : first_row + slot_count].astype(jnp.float32)
        segments = segment[first_row : first_row + slot_count]
        choices = expert_ids[first_row : first_row + slot_count]
        upstream = grad_out[first_row : first_row + slot_count].astype(jnp.float32)
        w_attn, gate_full, up_full, down_full = (
            lax.all_gather(attn_weight, "fsdp", axis=1, tiled=True),
            lax.all_gather(w_gate, "fsdp", axis=1, tiled=True),
            lax.all_gather(w_up, "fsdp", axis=1, tiled=True),
            lax.all_gather(w_down, "fsdp", axis=0, tiled=True),
        )
        scale_one = lax.rsqrt(jnp.mean(inputs * inputs, axis=-1, keepdims=True) + EPSILON)
        normed = (inputs * scale_one * norm_gains[0]).astype(jnp.bfloat16)
        triple = jnp.dot(
            normed, w_attn[:, :triple_width], preferred_element_type=jnp.float32
        ).astype(jnp.bfloat16)
        query = triple[:, :model_width].reshape(slot_count, head_count, head_width)
        keyset = triple[:, model_width : 2 * model_width].reshape(
            slot_count, head_count, head_width
        )
        valueset = triple[:, 2 * model_width :].reshape(slot_count, head_count, head_width)
        allowed = (segments[:, None] == segments[None, :]) & causal
        scores = masked_scores(query, keyset, offsets, allowed, factor)
        peak = jnp.max(scores, axis=-1, keepdims=True)
        log_total = peak + jnp.log(jnp.sum(jnp.exp(scores - peak), axis=-1, keepdims=True))
        weights_low = jnp.exp(scores - log_total).astype(jnp.bfloat16)
        mixed = jnp.einsum(
            "hij,jhd->ihd", weights_low, valueset, preferred_element_type=jnp.float32
        )
        mixed = mixed.reshape(slot_count, model_width).astype(jnp.bfloat16)
        branch = lax.dot_general(
            mixed, w_attn[:, triple_width:], contract_cols, preferred_element_type=jnp.float32
        )
        middle = inputs + branch
        scale_two = lax.rsqrt(jnp.mean(middle * middle, axis=-1, keepdims=True) + EPSILON)
        second = (middle * scale_two * norm_gains[1]).astype(jnp.bfloat16)
        second_wide = second.astype(jnp.float32)
        router_probs = jax.nn.softmax(jnp.dot(second_wide, router, precision=HIGHEST), axis=-1)
        picked = jnp.any(choices[:, :, None] == jnp.arange(routed_count)[None, None, :], axis=1)
        picked_f = jnp.where(picked, 1.0, 0.0)
        chosen_total = jnp.sum(router_probs * picked_f, axis=-1)
        active = jnp.where(segments >= 0, 1.0, 0.0)
        live = picked_f[:, 0] * active
        combine = router_probs[:, 0] * live / chosen_total
        gated = jnp.dot(second, gate_full, preferred_element_type=jnp.float32)
        lifted = jnp.dot(second, up_full, preferred_element_type=jnp.float32)
        activated, gelu_back = jax.vjp(gelu_tanh, gated)
        hidden = (activated * lifted).astype(jnp.bfloat16)
        expert_out = jnp.dot(hidden, down_full, preferred_element_type=jnp.float32)
        results.append((middle + combine[:, None] * expert_out).astype(jnp.bfloat16))
        d_expert = (combine[:, None] * upstream).astype(jnp.bfloat16)
        d_combine = jnp.sum(expert_out * upstream, axis=-1)
        d_hidden = lax.dot_general(
            d_expert, down_full, contract_cols, preferred_element_type=jnp.float32
        )
        d_gated = gelu_back(d_hidden * lifted)[0].astype(jnp.bfloat16)
        d_lifted = (d_hidden * activated).astype(jnp.bfloat16)
        d_gate_w = lax.dot_general(
            second, d_gated, contract_rows, preferred_element_type=jnp.float32
        )
        d_up_w = lax.dot_general(
            second, d_lifted, contract_rows, preferred_element_type=jnp.float32
        )
        d_down_w = lax.dot_general(
            hidden, d_expert, contract_rows, preferred_element_type=jnp.float32
        )
        d_second = lax.dot_general(
            d_gated, gate_full, contract_cols, preferred_element_type=jnp.float32
        )
        d_second = d_second + lax.dot_general(
            d_lifted, up_full, contract_cols, preferred_element_type=jnp.float32
        )
        ratio = router_probs[:, 0] / (chosen_total * chosen_total)
        d_probs = (d_combine * live)[:, None] * (
            first_hot[None, :] / chosen_total[:, None] - ratio[:, None] * picked_f
        )
        d_logits = router_probs * (
            d_probs - jnp.sum(d_probs * router_probs, axis=-1, keepdims=True)
        )
        grad_router = grad_router + jnp.dot(second_wide.T, d_logits, precision=HIGHEST)
        d_second = d_second + jnp.dot(d_logits, router.T, precision=HIGHEST)
        gain_two = jnp.sum(d_second * middle * scale_two, axis=0)
        d_middle = upstream + norm_back(middle, scale_two, norm_gains[1], d_second)
        d_branch = d_middle.astype(jnp.bfloat16)
        d_out_proj = lax.dot_general(
            d_branch, mixed, contract_rows, preferred_element_type=jnp.float32
        )
        d_mixed = jnp.dot(
            d_branch, w_attn[:, triple_width:], preferred_element_type=jnp.float32
        ).astype(jnp.bfloat16)
        d_mixed = d_mixed.reshape(slot_count, head_count, head_width)
        scores = masked_scores(query, keyset, offsets, allowed, factor)
        weights_full = jnp.exp(scores - log_total)
        weights_low = weights_full.astype(jnp.bfloat16)
        d_weights = jnp.einsum(
            "ihd,jhd->hij", d_mixed, valueset, preferred_element_type=jnp.float32
        )
        d_values = jnp.einsum(
            "hij,ihd->jhd", weights_low, d_mixed, preferred_element_type=jnp.float32
        )
        d_scores = weights_full * (
            d_weights - jnp.sum(weights_full * d_weights, axis=-1, keepdims=True)
        )
        d_scores = d_scores.astype(jnp.bfloat16)
        d_query = (
            jnp.einsum("hij,jhd->ihd", d_scores, keyset, preferred_element_type=jnp.float32)
            * factor
        )
        d_keys = (
            jnp.einsum("hij,ihd->jhd", d_scores, query, preferred_element_type=jnp.float32) * factor
        )
        grad_table = grad_table + jnp.einsum(
            "hij,ijb->bh", d_scores.astype(jnp.float32), bucket_hit, precision=HIGHEST
        )
        d_triple = jnp.concatenate(
            [
                d_query.reshape(slot_count, model_width),
                d_keys.reshape(slot_count, model_width),
                d_values.reshape(slot_count, model_width),
            ],
            axis=1,
        ).astype(jnp.bfloat16)
        d_in_proj = lax.dot_general(
            normed, d_triple, contract_rows, preferred_element_type=jnp.float32
        )
        d_normed = lax.dot_general(
            d_triple, w_attn[:, :triple_width], contract_cols, preferred_element_type=jnp.float32
        )
        gain_one = jnp.sum(d_normed * inputs * scale_one, axis=0)
        grad_gains = grad_gains + jnp.stack([gain_one, gain_two])
        input_grads.append(
            (d_middle + norm_back(inputs, scale_one, norm_gains[0], d_normed)).astype(jnp.bfloat16)
        )
        d_attn = jnp.concatenate([d_in_proj, d_out_proj], axis=1)
        current = (d_attn, d_gate_w, d_up_w, d_down_w)
        if local_sums is None:
            local_sums = current
        else:
            local_sums = tuple((held + fresh for held, fresh in zip(local_sums, current)))
    shares = (
        lax.psum_scatter(local_sums[0], "fsdp", scatter_dimension=1, tiled=True),
        lax.psum_scatter(local_sums[1], "fsdp", scatter_dimension=1, tiled=True),
        lax.psum_scatter(local_sums[2], "fsdp", scatter_dimension=1, tiled=True),
        lax.psum_scatter(local_sums[3], "fsdp", scatter_dimension=0, tiled=True),
    )
    attn_shard = shares[0]
    expert_shard = (shares[1], shares[2], shares[3])
    grad_gains, grad_table, grad_router = lax.psum((grad_gains, grad_table, grad_router), "fsdp")
    return (
        jnp.concatenate(results, axis=0),
        jnp.concatenate(input_grads, axis=0),
        attn_shard,
        expert_shard[0],
        expert_shard[1],
        expert_shard[2],
        grad_gains,
        grad_table,
        grad_router,
    )


def solution(mesh):
    in_specs = (
        P("fsdp", None),
        P(None, "fsdp"),
        P(None, "fsdp"),
        P(None, "fsdp"),
        P("fsdp", None),
        P(),
        P(),
        P(),
        P("fsdp", None),
        P("fsdp"),
        P("fsdp", None),
        P(),
    )
    out_specs = (
        P("fsdp", None),
        P("fsdp", None),
        P(None, "fsdp"),
        P(None, "fsdp"),
        P(None, "fsdp"),
        P("fsdp", None),
        P(),
        P(),
        P(),
    )
    return jax.shard_map(body, mesh=mesh, in_specs=in_specs, out_specs=out_specs, check_vma=False)
```

profile of v0, /device:TPU:0, one launch (start us, length us, event | category | flops | bytes accessed | tf_op | source)
XLA Modules:
  0.0 1025.0 jit_solution(11675155536634025900)
XLA Ops:
  11.3 24.7 %gather_fusion = s32[4096]{0:T(1024)S(1)} fusion(s32[64]{0:T(128)S(1)} %copy-done.2, s32[4096]{0:T(1024)S(1)} %broadcast_clamp_fusion), kind=kCustom, calls=%fused_computation | custom fusion | bytes 49152 | tf_op jit(solution)/shard_map/gather | solution.py:51
  37.7 39.6 %all-gather.5.cloned.1.call-done = bf16[768,3072]{0,1:T(8,128)(2,1)} async-done(((bf16[768,96]{0,1:T(8,128)(2,1)}), bf16[768,3072]{0,1:T(8,128)(2,1)}) %all-gather.5.cloned.1.call-update) | async-done | bytes 4718608 | tf_op jit(solution)/shard_map/all_gather | solution.py:76
  77.3 3.2 convolution_convert_fusion
  81.1 3.3 convolution_convert_fusion.1
  91.5 50.6 %all-gather.9.cloned.1.call-done = bf16[768,3072]{0,1:T(8,128)(2,1)} async-done(((bf16[768,96]{0,1:T(8,128)(2,1)}), bf16[768,3072]{0,1:T(8,128)(2,1)}) %all-gather.9.cloned.1.call-update) | async-done | bytes 4718608 | tf_op jit(solution)/shard_map/all_gather | solution.py:78
  142.2 4.9 fusion.135
  149.5 57.5 %all-gather.7.cloned.1.call-done = bf16[768,3072]{0,1:T(8,128)(2,1)} async-done(((bf16[768,96]{0,1:T(8,128)(2,1)}), bf16[768,3072]{0,1:T(8,128)(2,1)}) %all-gather.7.cloned.1.call-update) | async-done | bytes 4718608 | tf_op jit(solution)/shard_map/all_gather | solution.py:77
  207.0 4.9 fusion.134
  214.4 57.4 %all-gather.11.cloned.1.call-done = bf16[3072,768]{1,0:T(8,128)(2,1)} async-done(((bf16[96,768]{1,0:T(8,128)(2,1)}), bf16[3072,768]{1,0:T(8,128)(2,1)}) %all-gather.11.cloned.1.call-update) | async-done | bytes 4718608 | tf_op jit(solution)/shard_map/all_gather | solution.py:79
  271.8 4.5 multiply_convert_fusion
  303.1 2.8 fusion.84
  329.3 4.1 maximum_add_fusion
  333.4 9.7 copy.197
  345.6 5.1 convolution_add_fusion
  353.1 5.1 convolution_add_fusion.1
  360.7 5.1 convolution_add_fusion.2
  366.9 2.8 fusion
  369.7 2.9 fusion.66
  373.3 39.4 %all-reduce = (f32[2,768]{1,0:T(2,128)}, f32[32,12]{0,1:T(8,128)}) all-reduce(f32[2,768]{1,0:T(2,128)S(1)} %maximum_add_fusion.1, f32[32,12]{0,1:T(8,128)S(1)} %fusion.18), channel_id=1, replica_groups=mesh['fsdp'=32] {'fsdp'}, use_global_device_ids=true, to_apply=%region_34.35 | all-reduce | flops 1920 | bytes 15360 | tf_op jit(solution)/shard_map/psum | solution.py:217
  414.2 34.2 %all-reduce.3.cloned.1.call-done = f32[768,64]{0,1:T(8,128)} async-done(((f32[768,64]{0,1:T(8,128)}), f32[768,64]{0,1:T(8,128)}) %all-reduce.3.cloned.1.call-update) | async-done | bytes 196624 | tf_op jit(solution)/shard_map/psum | solution.py:217
  448.5 143.5 %reduce-scatter.13.cloned.1.call-done = f32[96,768]{1,0:T(8,128)} async-done(((f32[3072,768]{1,0:T(8,128)}), f32[96,768]{1,0:T(8,128)}) %reduce-scatter.13.cloned.1.call-update) | async-done | bytes 294928
  591.9 141.6 %reduce-scatter.11.cloned.1.call-done = f32[96,768]{1,0:T(8,128)} async-done(((f32[3072,768]{1,0:T(8,128)}), f32[96,768]{1,0:T(8,128)}) %reduce-scatter.11.cloned.1.call-update) | async-done | bytes 294928 | tf_op jit(solution)/shard_map/reduce_scatter | solution.py:213
  733.6 141.6 %reduce-scatter.9.cloned.1.call-done = f32[768,96]{0,1:T(8,128)} async-done(((f32[768,3072]{0,1:T(8,128)}), f32[768,96]{0,1:T(8,128)}) %reduce-scatter.9.cloned.1.call-update) | async-done | bytes 294928 | tf_op jit(solution)/shard_map/reduce_scatter | solution.py:212
  875.2 141.6 %reduce-scatter.7.cloned.1.call-done = f32[768,96]{0,1:T(8,128)} async-done(((f32[768,3072]{0,1:T(8,128)}), f32[768,96]{0,1:T(8,128)}) %reduce-scatter.7.cloned.1.call-update) | async-done | bytes 294928 | tf_op jit(solution)/shard_map/reduce_scatter | solution.py:211
  (299 shorter events, 79.6 us)
Async XLA Ops:
  7.2 83.0 %copy-start = (f32[768,64]{0,1:T(8,128)S(1)}, f32[768,64]{0,1:T(8,128)}, u32[]{:S(2)}) copy-start(f32[768,64]{0,1:T(8,128)} %param.19) | copy-start | bytes 589828
  7.2 70.1 %all-gather.5.cloned.1.call-start = ((), (), s32[]{:S(2)}) async-start(), calls=%async_computation.4 | async-start | bytes 4866048 | tf_op jit(solution)/shard_map/all_gather | solution.py:76
  7.9 134.2 %all-gather.9.cloned.1.call-start = ((), (), s32[]{:S(2)}) async-start(), calls=%async_computation.6 | async-start | bytes 4866048 | tf_op jit(solution)/shard_map/all_gather | solution.py:78
  8.7 198.3 %all-gather.7.cloned.1.call-start = ((), (), s32[]{:S(2)}) async-start(), calls=%async_computation.5 | async-start | bytes 4866048 | tf_op jit(solution)/shard_map/all_gather | solution.py:77
  9.4 262.3 %all-gather.11.cloned.1.call-start = ((), (), s32[]{:S(2)}) async-start(), calls=%async_computation.7 | async-start | bytes 4866048 | tf_op jit(solution)/shard_map/all_gather | solution.py:79
  10.0 438.5 %all-reduce.3.cloned.1.call-start = ((), (), s32[]{:S(2)}) async-start(), calls=%async_computation.11 | async-start | bytes 393216 | tf_op jit(solution)/shard_map/psum | solution.py:217
  11.1 274.2 %copy-start.47 = (pred[64,64]{0,1:T(32,128)(4,1)}, pred[64,64]{0,1:T(32,128)(4,1)S(1)}, u32[]{:S(2)}) copy-start(pred[64,64]{0,1:T(32,128)(4,1)S(1)} %copy.146) | copy-start | bytes 12292
  11.2 271.7 %copy-start.45 = (pred[64,64]{0,1:T(32,128)(4,1)}, pred[64,64]{0,1:T(32,128)(4,1)S(1)}, u32[]{:S(2)}) copy-start(pred[64,64]{0,1:T(32,128)(4,1)S(1)} %copy.151) | copy-start | bytes 12292
  37.6 46.8 %copy-start.62 = (f32[64]{0:T(128)}, f32[64]{0:T(128)S(1)}, u32[]{:S(2)}) copy-start(f32[64]{0:T(128)S(1)} %get-tuple-element.121) | copy-start | bytes 772
  87.9 59.2 %copy-start.44 = (f32[12,64]{1,0:T(8,128)}, f32[12,64]{1,0:T(8,128)S(1)}, u32[]{:S(2)}) copy-start(f32[12,64]{1,0:T(8,128)S(1)} %log_add_fusion) | copy-start | bytes 9220
  88.2 61.3 %copy-start.11 = (bf16[12,64,64]{2,1,0:T(8,128)(2,1)}, bf16[12,64,64]{2,1,0:T(8,128)(2,1)S(1)}, u32[]{:S(2)}) copy-start(bf16[12,64,64]{2,1,0:T(8,128)(2,1)S(1)} %convolution_convert_fusion.4) | copy-start | bytes 294916
  90.8 194.5 %copy-start.31 = (f32[64,64]{0,1:T(8,128)}, f32[64,64]{0,1:T(8,128)S(1)}, u32[]{:S(2)}) copy-start(f32[64,64]{0,1:T(8,128)S(1)} %get-tuple-element.66) | copy-start | bytes 49156
  90.8 194.5 %copy-start.54 = (f32[64]{0:T(128)}, f32[64]{0:T(128)S(1)}, u32[]{:S(2)}) copy-start(f32[64]{0:T(128)S(1)} %get-tuple-element.65) | copy-start | bytes 772
  91.4 191.4 %copy-start.30 = (f32[64,64]{0,1:T(8,128)}, f32[64,64]{0,1:T(8,128)S(1)}, u32[]{:S(2)}) copy-start(f32[64,64]{0,1:T(8,128)S(1)} %get-tuple-element.68) | copy-start | bytes 49156
  91.4 191.5 %copy-start.58 = (f32[64]{0:T(128)}, f32[64]{0:T(128)S(1)}, u32[]{:S(2)}) copy-start(f32[64]{0:T(128)S(1)} %get-tuple-element.67) | copy-start | bytes 772
  91.5 191.4 %copy-start.69 = (f32[64]{0:T(128)}, f32[64]{0:T(128)S(1)}, u32[]{:S(2)}) copy-start(f32[64]{0:T(128)S(1)} %fusion.116) | copy-start | bytes 772
  91.5 180.2 %copy-start.75 = (f32[64]{0:T(128)}, f32[64]{0:T(128)S(1)}, u32[]{:S(2)}) copy-start(f32[64]{0:T(128)S(1)} %get-tuple-element.98) | copy-start | bytes 772
  91.5 185.7 %copy-start.78 = (f32[64]{0:T(128)}, f32[64]{0:T(128)S(1)}, u32[]{:S(2)}) copy-start(f32[64]{0:T(128)S(1)} %get-tuple-element.97) | copy-start | bytes 772
  149.5 122.2 %copy-start.25 = (bf16[128,768]{1,0:T(8,128)(2,1)S(1)}, bf16[128,768]{1,0:T(8,128)(2,1)}, u32[]{:S(2)}) copy-start(bf16[128,768]{1,0:T(8,128)(2,1)} %param.20) | copy-start | bytes 589828
  325.3 266.6 %reduce-scatter.13.cloned.1.call-start = ((), (), s32[]{:S(2)}) async-start(), calls=%async_computation.12 | async-start | bytes 9732096
  343.1 390.4 %reduce-scatter.11.cloned.1.call-start = ((), (), s32[]{:S(2)}) async-start(), calls=%async_computation.10 | async-start | bytes 9732096 | tf_op jit(solution)/shard_map/reduce_scatter | solution.py:213
  350.7 524.5 %reduce-scatter.9.cloned.1.call-start = ((), (), s32[]{:S(2)}) async-start(), calls=%async_computation.9 | async-start | bytes 9732096 | tf_op jit(solution)/shard_map/reduce_scatter | solution.py:212
  358.3 658.5 %reduce-scatter.7.cloned.1.call-start = ((), (), s32[]{:S(2)}) async-start(), calls=%async_computation.8 | async-start | bytes 9732096 | tf_op jit(solution)/shard_map/reduce_scatter | solution.py:211
  366.9 651.6 %copy-start.1 = (f32[768,64]{0,1:T(8,128)S(1)}, f32[768,64]{0,1:T(8,128)}, u32[]{:S(2)}) copy-start(f32[768,64]{0,1:T(8,128)} %param.19) | copy-start | bytes 589828
  (70 other events, 518.2 us)
Sparse Core Ops, SparseCore 0:
  10.9 66.3 all-gather.4
  80.2 61.9 all-gather.8
  145.1 61.9 all-gather.6
  209.8 61.9 all-gather.10
  325.4 123.0 all-reduce.2
  454.8 137.0 reduce-scatter.12
  598.4 135.1 reduce-scatter.10
  740.0 135.1 reduce-scatter.8
  881.7 135.0 reduce-scatter.6
where the time goes:
time: 1030 us; the launch traced here: 1020 us
  waiting for transfers between devices  810 us (79%)
  matrix products  88.9 us (9%)
  local copies, waits for them, and re-layouts  61.1 us (6%)
  blocking collectives  39.4 us (4%)
  between operations  15.1 us (1%)
    unnamed x10, waiting for transfers between devices  146 us
    reduce_scatter x1, waiting for transfers between devices, body(): lax.psum_scatter(local_sums[2], 'fsdp', scatter_dimension=1, tiled=True)  142 us
    reduce_scatter x1, waiting for transfers between devices, body(): lax.psum_scatter(local_sums[1], 'fsdp', scatter_dimension=1, tiled=True)  142 us
    reduce_scatter x1, waiting for transfers between devices, body(): lax.psum_scatter(local_sums[3], 'fsdp', scatter_dimension=0, tiled=True)  142 us
    all_gather x1, waiting for transfers between devices, body(): lax.all_gather(w_gate, 'fsdp', axis=1, tiled=True)  57.5 us
    all_gather x1, waiting for transfers between devices, body(): lax.all_gather(w_down, 'fsdp', axis=0, tiled=True)  57.4 us
    all_gather x1, waiting for transfers between devices, body(): lax.all_gather(w_up, 'fsdp', axis=1, tiled=True)  50.6 us
    all_gather x1, waiting for transfers between devices, body(): lax.all_gather(attn_weight, 'fsdp', axis=1, tiled=True)  39.6 us
  transfers between devices with their start and end apart: 9, of which 9 were waited for; matrix products, arithmetic and copies ran while one was open for 10% of the time, Pallas kernels for 0%

commit v1 on v0

v1 whole, which is shorter than its diff:
```python
import functools
import jax
import jax.numpy as jnp
from jax import lax
from jax.experimental import pallas as pl
from jax.experimental.pallas import tpu as pltpu
from jax.sharding import PartitionSpec as P

EPSILON = 1e-06
HIGHEST = lax.Precision.HIGHEST
MESH = pl.DeviceIdType.MESH
TEAM = 4
F32 = jnp.float32
BF16 = jnp.bfloat16
VMEM = pl.BlockSpec(memory_space=pltpu.VMEM)
ANY = pl.BlockSpec(memory_space=pl.ANY)
CONTRACT_ROWS = (((0,), (0,)), ((), ()))
CONTRACT_COLS = (((1,), (1,)), ((), ()))


def place(n):
    sub = n // (TEAM * TEAM)
    me = lax.axis_index("fsdp")
    p = me // (TEAM * sub)
    t = lax.rem(me // sub, TEAM)
    s = lax.rem(me, sub)
    return sub, p, t, s, (lambda p, t, s: (p * (TEAM * sub) + t * sub + s,))


def greet(peers):
    barrier = pltpu.get_barrier_semaphore()
    for peer in peers:
        pl.semaphore_signal(barrier, inc=1, device_id=peer, device_id_type=MESH)
    pl.semaphore_wait(barrier, len(peers))


def remote(src, dst, send, recv, peer):
    return pltpu.make_async_remote_copy(
        src_ref=src, dst_ref=dst, send_sem=send, recv_sem=recv, device_id=peer, device_id_type=MESH
    )


def other(index, step, count):
    return lax.rem(index + step, count)


def gather_kernel(n, w_ref, tok_ref, dy_ref, meta_ref, w_all, tok_all, dy_all, meta_all,
                  p_send, p_recv, s_send, s_recv, t_send, t_recv, own_sem):
    sub, p, t, s, dev = place(n)
    peers = [dev(other(p, k, TEAM), t, s) for k in range(1, TEAM)]
    peers += [dev(p, t, other(s, k, sub)) for k in range(1, sub)]
    peers += [dev(p, other(t, k, TEAM), s) for k in range(1, TEAM)]
    greet(peers)
    copies = []
    for k in range(1, TEAM):
        c = remote(w_ref, w_all.at[:, p, s], p_send.at[k], p_recv.at[k], dev(other(p, k, TEAM), t, s))
        c.start()
        copies.append(c)
    for k in range(1, sub):
        c = remote(w_ref, w_all.at[:, p, s], s_send.at[0, k], s_recv.at[0, k], dev(p, t, other(s, k, sub)))
        c.start()
        copies.append(c)
    for i, (src, dst) in enumerate(((tok_ref, tok_all), (dy_ref, dy_all), (meta_ref, meta_all))):
        for k in range(1, TEAM):
            c = remote(src, dst.at[t], t_send.at[i, k], t_recv.at[i, k], dev(p, other(t, k, TEAM), s))
            c.start()
            copies.append(c)
    local = [pltpu.make_async_copy(w_ref, w_all.at[:, p, s], own_sem.at[0]),
             pltpu.make_async_copy(tok_ref, tok_all.at[t], own_sem.at[1]),
             pltpu.make_async_copy(dy_ref, dy_all.at[t], own_sem.at[2]),
             pltpu.make_async_copy(meta_ref, meta_all.at[t], own_sem.at[3])]
    for c in local:
        c.start()
    for k in range(1, TEAM):
        copies[k - 1].wait_recv()
        q = other(p, TEAM - k, TEAM)
        for j in range(1, sub):
            c = remote(w_all.at[:, q, s], w_all.at[:, q, s], s_send.at[k, j], s_recv.at[k, j],
                       dev(p, t, other(s, j, sub)))
            c.start()
            copies.append(c)
    for k in range(1, TEAM):
        copies[k - 1].wait_send()
    for c in copies[TEAM - 1:]:
        c.wait()
    for c in local:
        c.wait()


def gather(n, w, tok, dy, meta):
    sub = n // (TEAM * TEAM)
    dma = pltpu.SemaphoreType.DMA
    shape = jax.ShapeDtypeStruct
    return pl.pallas_call(
        functools.partial(gather_kernel, n),
        out_shape=(
            shape((w.shape[0], TEAM, sub) + w.shape[1:], BF16),
            shape((TEAM,) + tok.shape, BF16),
            shape((TEAM,) + dy.shape, BF16),
            shape((TEAM,) + meta.shape, jnp.int32),
        ),
        in_specs=[VMEM] * 4,
        out_specs=(ANY,) * 4,
        scratch_shapes=[dma((TEAM,)), dma((TEAM,)), dma((TEAM, sub)), dma((TEAM, sub)),
                        dma((3, TEAM)), dma((3, TEAM)), dma((4,))],
        compiler_params=pltpu.CompilerParams(collective_id=0, has_side_effects=True),
        name="gather_all",
    )(w, tok, dy, meta)


def middle_kernel(n, part_ref, x_ref, gain_ref, y_ref, h_all, got, held, a_send, a_recv, b_send, b_recv, own_sem):
    sub, p, t, s, dev = place(n)
    peers = [dev(p, other(t, k, TEAM), s) for k in range(1, TEAM)]
    greet(peers)
    copies = []
    for k in range(1, TEAM):
        u = other(t, k, TEAM)
        c = remote(part_ref.at[u], got.at[k - 1], a_send.at[k], a_recv.at[k], dev(p, u, s))
        c.start()
        copies.append(c)
    total = x_ref[...].astype(F32) + part_ref[t].astype(F32)
    for k in range(1, TEAM):
        copies[k - 1].wait_recv()
        total = total + got[k - 1].astype(F32)
    y_ref[...] = total
    scale = lax.rsqrt(jnp.mean(total * total, axis=-1, keepdims=True) + EPSILON)
    held[...] = (total * scale * gain_ref[1:2, :]).astype(BF16)
    local = pltpu.make_async_copy(held, h_all.at[t], own_sem)
    local.start()
    sends = []
    for k in range(1, TEAM):
        c = remote(held, h_all.at[t], b_send.at[k], b_recv.at[k], dev(p, other(t, k, TEAM), s))
        c.start()
        sends.append(c)
    for c in copies:
        c.wait_send()
    for c in sends:
        c.wait()
    local.wait()


def middle_exchange(n, part, x, gains):
    dma = pltpu.SemaphoreType.DMA
    shape = jax.ShapeDtypeStruct
    return pl.pallas_call(
        functools.partial(middle_kernel, n),
        out_shape=(shape(x.shape, F32), shape((TEAM,) + x.shape, BF16)),
        in_specs=[VMEM] * 3,
        out_specs=(VMEM, ANY),
        scratch_shapes=[pltpu.VMEM((TEAM - 1,) + x.shape, BF16), pltpu.VMEM(x.shape, BF16),
                        dma((TEAM,)), dma((TEAM,)), dma((TEAM,)), dma((TEAM,)), dma],
        compiler_params=pltpu.CompilerParams(collective_id=1, has_side_effects=True),
        name="middle_exchange",
    )(part, x, gains)


def reduce_kernel(n, m, *refs):
    parts, grad_ref = refs[:m], refs[m]
    outs, grad_out = refs[m + 1:2 * m + 1], refs[2 * m + 1]
    (got, sib, to_send, far, t_send, t_recv, s_send, s_recv, p_send, p_recv) = refs[2 * m + 2:]
    sub, p, t, s, dev = place(n)
    peers = [dev(other(p, k, TEAM), t, s) for k in range(1, TEAM)]
    peers += [dev(p, t, other(s, k, sub)) for k in range(1, sub)]
    peers += [dev(p, other(t, k, TEAM), s) for k in range(1, TEAM)]
    greet(peers)
    kinds = grad_ref.shape[0]
    near, tokens, wide = [], [], []
    for k in range(1, sub):
        v = other(s, k, sub)
        c = remote(grad_ref.at[:, :, v], sib.at[k - 1], s_send.at[k], s_recv.at[k], dev(p, t, v))
        c.start()
        near.append(c)
    for i in range(m):
        for k in range(1, TEAM):
            u = other(t, k, TEAM)
            c = remote(parts[i].at[u], got.at[i, k - 1], t_send.at[i, k], t_recv.at[i, k], dev(p, u, s))
            c.start()
            tokens.append(c)
    for c in near:
        c.wait_recv()
    for k in range(1, TEAM):
        q = other(p, k, TEAM)

        def fold(kind, carry, q=q, k=k):
            total = grad_ref[kind, q, s].astype(F32)
            for j in range(1, sub):
                total = total + sib[j - 1, kind, q].astype(F32)
            to_send[k - 1, kind] = total.astype(BF16)
            return carry

        lax.fori_loop(0, kinds, fold, 0)
        c = remote(to_send.at[k - 1], far.at[k - 1], p_send.at[k], p_recv.at[k], dev(q, t, s))
        c.start()
        wide.append(c)
    for i in range(m):
        total = parts[i][t].astype(F32)
        for k in range(1, TEAM):
            tokens[i * (TEAM - 1) + k - 1].wait_recv()
            total = total + got[i, k - 1].astype(F32)
        outs[i][...] = total
    for c in wide:
        c.wait_recv()

    def finish(kind, carry):
        total = grad_ref[kind, p, s].astype(F32)
        for j in range(1, sub):
            total = total + sib[j - 1, kind, p].astype(F32)
        for k in range(1, TEAM):
            total = total + far[k - 1, kind].astype(F32)
        grad_out[kind] = total
        return carry

    lax.fori_loop(0, kinds, finish, 0)
    for c in near + tokens + wide:
        c.wait_send()


def reduce_exchange(n, parts, grads, ident):
    sub = n // (TEAM * TEAM)
    m = len(parts)
    dma = pltpu.SemaphoreType.DMA
    shape = jax.ShapeDtypeStruct
    block = parts[0].shape[1:]
    kinds, tile = grads.shape[0], grads.shape[3:]
    outs = pl.pallas_call(
        functools.partial(reduce_kernel, n, m),
        out_shape=(shape(block, F32),) * m + (shape((kinds,) + tile, F32),),
        in_specs=[VMEM] * (m + 1),
        out_specs=(VMEM,) * (m + 1),
        scratch_shapes=[
            pltpu.VMEM((m, TEAM - 1) + block, BF16),
            pltpu.VMEM((sub - 1, kinds, TEAM) + tile, BF16),
            pltpu.VMEM((TEAM - 1, kinds) + tile, BF16),
            pltpu.VMEM((TEAM - 1, kinds) + tile, BF16),
            dma((m, TEAM)), dma((m, TEAM)), dma((sub,)), dma((sub,)), dma((TEAM,)), dma((TEAM,)),
        ],
        compiler_params=pltpu.CompilerParams(collective_id=ident, has_side_effects=True),
        name=f"reduce_{ident}",
    )(*parts, grads)
    return outs[:m], outs[m]


def share_kernel(n, x_ref, out, send, recv, own_sem):
    sub, p, t, s, dev = place(n)
    peers = [dev(p, other(t, k, TEAM), s) for k in range(1, TEAM)]
    greet(peers)
    local = pltpu.make_async_copy(x_ref, out.at[t], own_sem)
    local.start()
    copies = []
    for k in range(1, TEAM):
        c = remote(x_ref, out.at[t], send.at[k], recv.at[k], peers[k - 1])
        c.start()
        copies.append(c)
    for c in copies:
        c.wait()
    local.wait()


def share(n, x):
    dma = pltpu.SemaphoreType.DMA
    return pl.pallas_call(
        functools.partial(share_kernel, n),
        out_shape=jax.ShapeDtypeStruct((TEAM,) + x.shape, x.dtype),
        in_specs=[VMEM],
        out_specs=ANY,
        scratch_shapes=[dma((TEAM,)), dma((TEAM,)), dma],
        compiler_params=pltpu.CompilerParams(collective_id=3, has_side_effects=True),
        name="share_rows",
    )(x)


def small_kernel(n, x_ref, out_ref, got, mine, far, a_send, a_recv, b_send, b_recv, c_send, c_recv):
    sub, p, t, s, dev = place(n)
    team = [dev(p, other(t, k, TEAM), s) for k in range(1, TEAM)]
    count = TEAM * sub
    own = p * sub + s
    ring = []
    for k in range(1, count):
        v = other(own, k, count)
        ring.append(dev(v // sub, t, lax.rem(v, sub)))
    greet(team + ring)
    first, second, third = [], [], []
    for k in range(1, TEAM):
        c = remote(x_ref.at[other(t, k, TEAM)], got.at[k - 1], a_send.at[k], a_recv.at[k], team[k - 1])
        c.start()
        first.append(c)
    total = x_ref[t]
    for k in range(1, TEAM):
        first[k - 1].wait_recv()
        total = total + got[k - 1]
    mine[...] = total
    for k in range(1, count):
        c = remote(mine, far.at[own], b_send.at[k], b_recv.at[k], ring[k - 1])
        c.start()
        second.append(c)
    far[own] = total
    for c in second:
        c.wait_recv()
    summed = far[0]
    for k in range(1, count):
        summed = summed + far[k]
    out_ref[t] = summed
    for k in range(1, TEAM):
        c = remote(out_ref.at[t], out_ref.at[t], c_send.at[k], c_recv.at[k], team[k - 1])
        c.start()
        third.append(c)
    for c in first + second:
        c.wait_send()
    for c in third:
        c.wait()


def small_sum(n, x):
    count = n // TEAM
    dma = pltpu.SemaphoreType.DMA
    tile = x.shape[1:]
    return pl.pallas_call(
        functools.partial(small_kernel, n),
        out_shape=jax.ShapeDtypeStruct(x.shape, F32),
        in_specs=[VMEM],
        out_specs=VMEM,
        scratch_shapes=[pltpu.VMEM((TEAM - 1,) + tile, F32), pltpu.VMEM(tile, F32), pltpu.VMEM((count,) + tile, F32),
                        dma((TEAM,)), dma((TEAM,)), dma((count,)), dma((count,)), dma((TEAM,)), dma((TEAM,))],
        compiler_params=pltpu.CompilerParams(collective_id=5, has_side_effects=True),
        name="small_sum",
    )(x)


def gelu_tanh(inner):
    return jax.nn.gelu(inner, approximate=True)


def norm_back(inputs, scale, gain, upstream):
    weighted = gain * upstream
    return scale * weighted - inputs * scale * scale * scale * jnp.mean(
        weighted * inputs, axis=-1, keepdims=True
    )


def dot_t(a, b):
    return lax.dot_general(a, b, CONTRACT_COLS, preferred_element_type=F32)


def dot_r(a, b):
    return lax.dot_general(a, b, CONTRACT_ROWS, preferred_element_type=F32)


def dot(a, b):
    return jnp.dot(a, b, preferred_element_type=F32)


def body(n, tokens, attn_weight, w_gate, w_up, w_down, norm_gains, bias_table, router,
         grad_out, segment, expert_ids, bucket_of):
    rows, width = tokens.shape
    slots = bucket_of.shape[0]
    routed = router.shape[1]
    buckets, head_count = bias_table.shape
    head_width = width // head_count
    factor = head_width ** (-0.5)
    heads = head_count // TEAM
    part = heads * head_width
    sub, _, t, _, _ = place(n)
    all_rows = TEAM * rows
    spans = all_rows // slots

    w_local = jnp.stack([attn_weight.T, w_gate.T, w_up.T, w_down])
    meta = jnp.concatenate([segment[None], expert_ids.T, jnp.zeros((5, rows), jnp.int32)], axis=0)
    w_all, tok_all, dy_all, meta_all = gather(n, w_local, tokens, grad_out, meta)
    w_all = w_all.reshape(4, -1, width)
    attn_t, gate_t, up_t, down = w_all[0], w_all[1], w_all[2], w_all[3]
    qkv_t, out_t = attn_t[: 3 * part], attn_t[3 * part :]
    inputs = tok_all.reshape(all_rows, width).astype(F32)
    segments = meta_all[:, 0, :].reshape(all_rows)
    id_a = meta_all[:, 1, :].reshape(all_rows)
    id_b = meta_all[:, 2, :].reshape(all_rows)

    places = jnp.arange(slots)
    gap = places[:, None] - places[None, :]
    causal = gap >= 0
    gap_hit = (gap[:, :, None] == places[None, None, :]).astype(F32)
    bucket_hit = (bucket_of[:, None] == jnp.arange(buckets)[None, :]).astype(F32)
    table_mine = lax.dynamic_slice(bias_table, (0, heads * t), (buckets, heads))
    by_gap = jnp.dot(bucket_hit, table_mine, precision=HIGHEST)
    offsets = jnp.einsum("ijd,dh->hij", gap_hit, by_gap, precision=HIGHEST)

    scale_one = lax.rsqrt(jnp.mean(inputs * inputs, axis=-1, keepdims=True) + EPSILON)
    normed = (inputs * scale_one * norm_gains[0]).astype(BF16)
    triple = dot_t(normed, qkv_t).astype(BF16)
    heads_of = lambda v: v.reshape(spans, slots, heads, head_width)
    query = heads_of(triple[:, :part])
    keyset = heads_of(triple[:, part : 2 * part])
    valueset = heads_of(triple[:, 2 * part :])
    seg = segments.reshape(spans, slots)
    allowed = (seg[:, :, None] == seg[:, None, :]) & causal[None]
    raw = jnp.einsum("bihd,bjhd->bhij", query, keyset, preferred_element_type=F32)
    scores = jnp.where(allowed[:, None], raw * factor + offsets[None], -1e30)
    peak = jnp.max(scores, axis=-1, keepdims=True)
    lifted_scores = jnp.exp(scores - peak)
    weights = lifted_scores / jnp.sum(lifted_scores, axis=-1, keepdims=True)
    weights_low = weights.astype(BF16)
    mixed = jnp.einsum("bhij,bjhd->bihd", weights_low, valueset, preferred_element_type=F32)
    mixed = mixed.reshape(all_rows, part).astype(BF16)
    branch = dot(mixed, out_t).astype(BF16).reshape(TEAM, rows, width)
    middle, second_all = middle_exchange(n, branch, tokens, norm_gains)
    second_all = second_all.reshape(all_rows, width)

    second_wide = second_all.astype(F32)
    probs_all = jax.nn.softmax(jnp.dot(second_wide, router, precision=HIGHEST), axis=-1)
    lanes = jnp.arange(routed)[None, :]
    picked_all = jnp.where((id_a[:, None] == lanes) | (id_b[:, None] == lanes), 1.0, 0.0)
    total_all = jnp.sum(probs_all * picked_all, axis=-1)
    live_all = picked_all[:, 0] * jnp.where(segments >= 0, 1.0, 0.0)
    combine_all = probs_all[:, 0] * live_all / total_all
    gated = dot_t(second_all, gate_t)
    lifted = dot_t(second_all, up_t)
    activated, gelu_back = jax.vjp(gelu_tanh, gated)
    hidden = (activated * lifted).astype(BF16)
    out_part = dot(hidden, down).astype(BF16).reshape(TEAM, rows, width)
    d_expert = (combine_all[:, None] * dy_all.reshape(all_rows, width).astype(F32)).astype(BF16)
    d_hidden = dot_t(d_expert, down)
    d_gated = gelu_back(d_hidden * lifted)[0].astype(BF16)
    d_lifted = (d_hidden * activated).astype(BF16)
    back_part = (dot(d_gated, gate_t) + dot(d_lifted, up_t)).astype(BF16).reshape(TEAM, rows, width)
    grad_ffn = jnp.stack(
        [dot_r(d_gated, second_all).astype(BF16), dot_r(d_lifted, second_all).astype(BF16),
         dot_r(hidden, d_expert).astype(BF16)]
    ).reshape(3, TEAM, sub, -1, width)
    (expert_out, d_second), g_ffn = reduce_exchange(n, (out_part, back_part), grad_ffn, 2)

    mine = lambda v: lax.dynamic_slice_in_dim(v, t * rows, rows, 0)
    second, probs, picked = mine(second_wide), mine(probs_all), mine(picked_all)
    chosen_total, live, combine = mine(total_all), mine(live_all), mine(combine_all)
    upstream = grad_out.astype(F32)
    result = (middle + combine[:, None] * expert_out).astype(BF16)
    d_combine = jnp.sum(expert_out * upstream, axis=-1)
    first_hot = jnp.where(jnp.arange(routed) == 0, 1.0, 0.0)
    ratio = probs[:, 0] / (chosen_total * chosen_total)
    d_probs = (d_combine * live)[:, None] * (
        first_hot[None, :] / chosen_total[:, None] - ratio[:, None] * picked
    )
    d_logits = probs * (d_probs - jnp.sum(d_probs * probs, axis=-1, keepdims=True))
    grad_router_t = lax.dot_general(d_logits, second, CONTRACT_ROWS, precision=HIGHEST)
    d_second = d_second + jnp.dot(d_logits, router.T, precision=HIGHEST)
    scale_two = lax.rsqrt(jnp.mean(middle * middle, axis=-1, keepdims=True) + EPSILON)
    gain_two = jnp.sum(d_second * middle * scale_two, axis=0)
    d_middle = upstream + norm_back(middle, scale_two, norm_gains[1], d_second)
    d_branch = share(n, d_middle.astype(BF16)).reshape(all_rows, width)

    grad_out_t = dot_r(mixed, d_branch)
    d_mixed = heads_of(dot_t(d_branch, out_t).astype(BF16))
    d_weights = jnp.einsum("bihd,bjhd->bhij", d_mixed, valueset, preferred_element_type=F32)
    d_values = jnp.einsum("bhij,bihd->bjhd", weights_low, d_mixed, preferred_element_type=F32)
    d_scores = weights * (d_weights - jnp.sum(weights * d_weights, axis=-1, keepdims=True))
    d_scores = d_scores.astype(BF16)
    d_query = jnp.einsum("bhij,bjhd->bihd", d_scores, keyset, preferred_element_type=F32) * factor
    d_keys = jnp.einsum("bhij,bihd->bjhd", d_scores, query, preferred_element_type=F32) * factor
    score_sum = jnp.sum(d_scores.astype(F32), axis=0)
    gap_sum = jnp.einsum("hij,ijd->dh", score_sum, gap_hit, precision=HIGHEST)
    table_part = lax.dot_general(bucket_hit, gap_sum, CONTRACT_ROWS, precision=HIGHEST)
    grad_table = lax.dynamic_update_slice(jnp.zeros(bias_table.shape, F32), table_part, (0, heads * t))
    flat = lambda v: v.reshape(all_rows, part).astype(BF16)
    d_triple = jnp.concatenate([flat(d_query), flat(d_keys), flat(d_values)], axis=1)
    grad_in_t = dot_r(d_triple, normed)
    grad_attn = jnp.concatenate([grad_in_t, grad_out_t], axis=0).astype(BF16)
    grad_attn = grad_attn.reshape(1, TEAM, sub, -1, width)
    d_normed_part = dot(d_triple, qkv_t).astype(BF16).reshape(TEAM, rows, width)
    (d_normed,), g_attn = reduce_exchange(n, (d_normed_part,), grad_attn, 4)

    own_inputs = tokens.astype(F32)
    own_scale = mine(scale_one)
    gain_one = jnp.sum(d_normed * own_inputs * own_scale, axis=0)
    input_grad = (d_middle + norm_back(own_inputs, own_scale, norm_gains[0], d_normed)).astype(BF16)
    table_flat = grad_table.reshape(-1)
    lines = -(-table_flat.shape[0] // width)
    table_rows = jnp.pad(table_flat, (0, lines * width - table_flat.shape[0])).reshape(lines, width)
    small = jnp.concatenate([grad_router_t, gain_one[None], gain_two[None], table_rows], axis=0)
    depth = -(-small.shape[0] // (8 * TEAM)) * 8
    small = jnp.pad(small, ((0, depth * TEAM - small.shape[0]), (0, 0))).reshape(TEAM, depth, width)
    small = small_sum(n, small).reshape(TEAM * depth, width)
    grad_router = small[:routed].T
    grad_gains = small[routed : routed + 2]
    grad_table = small[routed + 2 : routed + 2 + lines].reshape(-1)[: table_flat.shape[0]].reshape(bias_table.shape)
    return (result, input_grad, g_attn[0].T, g_ffn[0].T, g_ffn[1].T, g_ffn[2],
            grad_gains, grad_table, grad_router)


def solution(mesh):
    n = mesh.shape["fsdp"]
    row, col = P("fsdp", None), P(None, "fsdp")
    in_specs = (row, col, col, col, row, P(), P(), P(), row, P("fsdp"), row, P())
    out_specs = (row, row, col, col, col, row, P(), P(), P())
    return jax.shard_map(
        functools.partial(body, n), mesh=mesh, in_specs=in_specs, out_specs=out_specs, check_vma=False
    )
```

time: 1030 us -> 279 us (0.27)
  waiting for transfers between devices: 810 us -> 0 us
  Pallas kernels: 0 us -> 194 us
  matrix products: 88.9 us -> 34.4 us
  blocking collectives: 39.4 us -> 0 us
  local copies, waits for them, and re-layouts: 61.1 us -> 24.9 us
  between operations: 15.1 us -> 1.39 us
  other arithmetic: 9.54 us -> 21.1 us
    reduce_scatter x3 -> x0, waiting for transfers between devices: 425 us -> none  [the longest x1 142 us: body(): lax.psum_scatter(local_sums[2], 'fsdp', scatter_dimension=1, tiled=True)]
    all_gather x4 -> x0, waiting for transfers between devices: 205 us -> none  [the longest x1 57.5 us: body(): lax.all_gather(w_gate, 'fsdp', axis=1, tiled=True)]
    pallas_call x0 -> x6, Pallas kernels: none -> 194 us  [the longest x2 78.3 us: reduce_exchange(): pl.pallas_call(functools.partial(reduce_kernel, n, m), out_shape=(shape(b...]
    unnamed x10 -> x0, waiting for transfers between devices: 146 us -> none
    dot_general x47 -> x26, matrix products: 86.8 us -> 30.7 us  [the longest x5 7.19 us: dot(): return jnp.dot(a, b, preferred_element_type=F32)]
    psum x1 -> x0, blocking collectives: 39.4 us -> none  [body(): lax.psum((grad_gains, grad_table, grad_router), 'fsdp')]
    psum x1 -> x0, waiting for transfers between devices: 34.2 us -> none  [body(): lax.psum((grad_gains, grad_table, grad_router), 'fsdp')]
    gather x2 -> x0, local copies, waits for them, and re-layouts: 24.8 us -> none  [body(): bucket_of[distance][:, :, None]]
  transfers between devices with their start and end apart: 9 -> 0, of which waited for: 9 -> 0; matrix products, arithmetic and copies ran while one was open for 10% -> 0% of each run, Pallas kernels for 0% -> 0%
where the time goes in v1:
time: 279 us; the launch traced here: 276 us
  Pallas kernels  194 us (70%)
  matrix products  34.4 us (12%)
  local copies, waits for them, and re-layouts  24.9 us (9%)
  other arithmetic  21.1 us (8%)
    pallas_call x2, Pallas kernels, reduce_exchange(): pl.pallas_call(functools.partial(reduce_kernel, n, m), out_shape=(shape(b...  78.3 us
    pallas_call x1, Pallas kernels, gather(): pl.pallas_call(functools.partial(gather_kernel, n), out_shape=(shape((w.s...  50.5 us
    pallas_call x1, Pallas kernels, small_sum(): pl.pallas_call(functools.partial(small_kernel, n), out_shape=jax.ShapeDty...  27.5 us
    pallas_call x1, Pallas kernels, middle_exchange(): pl.pallas_call(functools.partial(middle_kernel, n), out_shape=(shape(x.sh...  24.2 us
    pallas_call x1, Pallas kernels, share(): pl.pallas_call(functools.partial(share_kernel, n), out_shape=jax.ShapeDty...  13.5 us
    dot_general x5, matrix products, dot(): return jnp.dot(a, b, preferred_element_type=F32)  7.19 us
    dot_general x5, matrix products, dot_t(): return lax.dot_general(a, b, CONTRACT_COLS, preferred_element_type=F32)  5.64 us

profile of v1, /device:TPU:0, one launch (start us, length us, event | category | flops | bytes accessed | tf_op | source)
XLA Modules:
  0.0 276.0 jit_solution(8682975431379635518)
XLA Ops:
  4.0 2.8 %fusion.2 = f32[3,64,64]{2,0,1:T(4,128)S(1)} fusion(f32[64,3,1]{0,1,2:T(4,128)S(1)} %convolution_bitcast_fusion, s32[64,64]{1,0:T(8,128)S(1)} %iota_subtract_fusion), kind=kOutput, calls=%fused_computation.6 | convolution fusion | flops 9699328 | bytes 66304 | tf_op jit(solution)/shard_map/ijd,dh->hij/dot_general | solution.py:384
  6.9 2.1 pad_maximum_fusion.2.w_ref
  9.0 50.5 %gather_all.1 = (bf16[4,4,2,96,768]{4,3,2,1,0:T(8,128)(2,1)}, bf16[4,128,768]{2,1,0:T(8,128)(2,1)}, bf16[4,128,768]{2,1,0:T(8,128)(2,1)}, s32[4,8,128]{2,1,0:T(8,128)}) custom-call(bf16[4,96,768]{2,1,0:T(8,128)(2,1)} %pad_maximum_fusion.2.w_ref, bf16[128,768]{1,0:T(8,128)(2,1)} %x_ref.1, bf16[128,768]{1,0:T(8,128)(2,1)} %dy_ref.1, s32[8,128]{1,0:T(8,128)} %add_add_fusion.meta_ref), custom_call_target="tpu_custom_call" | custom-call | tf_op jit(solution)/shard_map/gather_all/pallas_call | solution.py:94
  59.5 1.4 multiply_reduce_fusion
  65.8 4.2 %fusion.71 = (bf16[1,4,2,96,768]{4,3,2,1,0:T(8,128)(2,1)}, bf16[1,4,2,96,768]{4,3,2,1,0:T(8,128)(2,1)}, bf16[1,4,2,96,768]{4,3,2,1,0:T(8,128)(2,1)}) fusion(bf16[4,4,2,96,768]{4,3,2,1,0:T(8,128)(2,1)} %get-tuple-element.21), kind=kLoop, calls=%fused_computation.150 | loop fusion | bytes 7077888 | tf_op jit(solution)/shard_map/slice | solution.py:370
  72.7 1.4 fusion.76
  74.2 2.2 fusion.19
  79.2 24.2 %middle_exchange.1 = (f32[128,768]{1,0:T(8,128)}, bf16[4,128,768]{2,1,0:T(8,128)(2,1)}) custom-call(bf16[4,128,768]{2,1,0:T(8,128)(2,1)} %bitcast.161, bf16[128,768]{1,0:T(8,128)(2,1)} %x_ref.1, f32[2,768]{1,0:T(2,128)} %gain_ref.1), custom_call_target="tpu_custom_call" | custom-call | tf_op jit(solution)/shard_map/middle_exchange/pallas_call | solution.py:145
  104.5 2.0 fusion.77
  113.0 1.8 multiply_convert_fusion
  114.8 1.7 convolution_convert_fusion.4
  117.3 1.7 add_convert_fusion
  121.4 2.0 pad_maximum_fusion.refs_2_
  123.4 52.0 %reduce_2.1 = (f32[128,768]{1,0:T(8,128)}, f32[128,768]{1,0:T(8,128)}, f32[3,96,768]{2,1,0:T(8,128)}) custom-call(bf16[4,128,768]{2,1,0:T(8,128)(2,1)} %bitcast.185, bf16[4,128,768]{2,1,0:T(8,128)(2,1)} %bitcast.186, bf16[3,4,2,96,768]{4,3,2,1,0:T(8,128)(2,1)} %pad_maximum_fusion.refs_2_), custom_call_target="tpu_custom_call" | custom-call | tf_op jit(solution)/shard_map/reduce_2/pallas_call | solution.py:225
  178.0 1.7 multiply_reduce_fusion.2
  180.6 13.5 %share_rows.1 = bf16[4,128,768]{2,1,0:T(8,128)(2,1)} custom-call(bf16[128,768]{1,0:T(8,128)(2,1)} %fusion.69.x_ref), custom_call_target="tpu_custom_call" | custom-call | tf_op jit(solution)/shard_map/share_rows/pallas_call | solution.py:261
  194.1 1.5 convolution_convert_fusion.11
  195.7 1.5 convolution_convert_fusion.10
  198.2 2.6 fusion.20
  208.5 1.7 convolution_convert_fusion.5
  212.0 26.3 %reduce_4.1 = (f32[128,768]{1,0:T(8,128)}, f32[1,96,768]{2,1,0:T(8,128)}) custom-call(bf16[4,128,768]{2,1,0:T(8,128)(2,1)} %bitcast.189, bf16[1,4,2,96,768]{4,3,2,1,0:T(8,128)(2,1)} %bitcast.160), custom_call_target="tpu_custom_call" | custom-call | tf_op jit(solution)/shard_map/reduce_4/pallas_call | solution.py:225
  239.5 2.1 fusion.32
  242.4 27.5 %small_sum.1 = f32[4,24,768]{2,1,0:T(8,128)} custom-call(f32[4,24,768]{2,1,0:T(8,128)} %bitcast.179), custom_call_target="tpu_custom_call" | custom-call | tf_op jit(solution)/shard_map/small_sum/pallas_call | solution.py:317
  271.9 1.6 slice_bitcast_fusion.3
  (147 shorter events, 44.5 us)
Async XLA Ops:
  0.6 103.8 %copy-start = (f32[768,64]{0,1:T(8,128)S(1)}, f32[768,64]{0,1:T(8,128)}, u32[]{:S(2)}) copy-start(f32[768,64]{0,1:T(8,128)} %param.19) | copy-start | bytes 589828
  4.0 57.0 %copy-start.24 = (s32[64,64]{1,0:T(8,128)}, s32[64,64]{1,0:T(8,128)S(1)}, u32[]{:S(2)}) copy-start(s32[64,64]{1,0:T(8,128)S(1)} %iota_subtract_fusion) | copy-start | bytes 49156
  59.5 4.8 %copy-start.1 = (bf16[4,128,768]{2,1,0:T(8,128)(2,1)S(1)}, bf16[4,128,768]{2,1,0:T(8,128)(2,1)}, u32[]{:S(2)}) copy-start(bf16[4,128,768]{2,1,0:T(8,128)(2,1)} %get-tuple-element.20) | copy-start | bytes 2359300
  65.8 4.2 %copy-start.13 = (bf16[1,3,2,96,768]{4,3,2,1,0:T(8,128)(2,1)}, bf16[1,3,2,96,768]{4,3,2,1,0:T(8,128)(2,1)S(1)}, u32[]{:S(2)}) copy-start(bf16[1,3,2,96,768]{4,3,2,1,0:T(8,128)(2,1)S(1)} %slice.84) | copy-start | bytes 2654212
  71.1 1.3 copy-start.6
  72.7 1.5 copy-start.16
  74.2 128.1 %copy-start.23 = (f32[8,3,64]{2,1,0:T(4,128)}, f32[8,3,64]{2,1,0:T(4,128)S(1)}, u32[]{:S(2)}) copy-start(f32[8,3,64]{2,1,0:T(4,128)S(1)} %get-tuple-element.86) | copy-start | bytes 18436
  79.2 28.9 %copy-start.3 = (bf16[4,128,768]{2,1,0:T(8,128)(2,1)S(1)}, bf16[4,128,768]{2,1,0:T(8,128)(2,1)}, u32[]{:S(2)}) copy-start(bf16[4,128,768]{2,1,0:T(8,128)(2,1)} %get-tuple-element.25) | copy-start | bytes 2359300
  108.1 1.4 copy-start.10
  123.4 52.0 %copy-start.5 = (bf16[128,768]{1,0:T(8,128)(2,1)S(1)}, bf16[128,768]{1,0:T(8,128)(2,1)}, u32[]{:S(2)}) copy-start(bf16[128,768]{1,0:T(8,128)(2,1)} %dy_ref.1) | copy-start | bytes 589828
  123.4 53.2 %copy-start.19 = (f32[512,64]{0,1:T(8,128)S(1)}, f32[512,64]{0,1:T(8,128)}, u32[]{:S(2)}) copy-start(f32[512,64]{0,1:T(8,128)} %copy-done.18) | copy-start | bytes 393220
  123.4 53.2 %copy-start.21 = (f32[512,64]{0,1:T(8,128)S(1)}, f32[512,64]{0,1:T(8,128)}, u32[]{:S(2)}) copy-start(f32[512,64]{0,1:T(8,128)} %copy-done.20) | copy-start | bytes 393220
  123.4 54.6 %copy-start.2 = (f32[128,768]{1,0:T(8,128)S(1)}, f32[128,768]{1,0:T(8,128)}, u32[]{:S(2)}) copy-start(f32[128,768]{1,0:T(8,128)} %get-tuple-element.23) | copy-start | bytes 1179652
  179.7 16.0 %copy-start.27 = (f32[128]{0:T(128)}, f32[128]{0:T(128)S(1)}, u32[]{:S(2)}) copy-start(f32[128]{0:T(128)S(1)} %broadcast_multiply_fusion.1) | copy-start | bytes 1540
  205.8 2.0 copy-start.30
  206.6 1.9 copy-start.14
  208.5 1.7 copy-start.17
  211.9 26.3 %copy-start.4 = (bf16[128,768]{1,0:T(8,128)(2,1)S(1)}, bf16[128,768]{1,0:T(8,128)(2,1)}, u32[]{:S(2)}) copy-start(bf16[128,768]{1,0:T(8,128)(2,1)} %x_ref.1) | copy-start | bytes 589828
  211.9 26.3 %copy-start.26 = (f32[128]{0:T(128)S(1)}, f32[128]{0:T(128)}, u32[]{:S(2)}) copy-start(f32[128]{0:T(128)} %fusion.63) | copy-start | bytes 1540
  211.9 27.5 %copy-start.8 = (f32[128,768]{1,0:T(8,128)S(1)}, f32[128,768]{1,0:T(8,128)}, u32[]{:S(2)}) copy-start(f32[128,768]{1,0:T(8,128)} %get-tuple-element.26) | copy-start | bytes 1179652
  211.9 27.5 %copy-start.28 = (f32[128]{0:T(128)S(1)}, f32[128]{0:T(128)}, u32[]{:S(2)}) copy-start(f32[128]{0:T(128)} %copy-done.27) | copy-start | bytes 1540
  211.9 27.5 %copy-start.29 = (f32[128]{0:T(128)S(1)}, f32[128]{0:T(128)}, u32[]{:S(2)}) copy-start(f32[128]{0:T(128)} %dynamic_slice.25) | copy-start | bytes 1540
  239.5 34.8 %copy-start.15 = (f32[3,96,768]{2,1,0:T(8,128)S(1)}, f32[3,96,768]{2,1,0:T(8,128)}, u32[]{:S(2)}) copy-start(f32[3,96,768]{2,1,0:T(8,128)} %get-tuple-element.30) | copy-start | bytes 2654212
  241.6 33.6 %copy-start.22 = (f32[1,96,768]{2,1,0:T(8,128)S(1)}, f32[1,96,768]{2,1,0:T(8,128)}, u32[]{:S(2)}) copy-start(f32[1,96,768]{2,1,0:T(8,128)} %get-tuple-element.29) | copy-start | bytes 884740
  (7 other events, 7.7 us)

commit v2 on v1

v2 whole, which is shorter than its diff:
```python
import functools
import jax
import jax.numpy as jnp
from jax import lax
from jax.experimental import pallas as pl
from jax.experimental.pallas import tpu as pltpu
from jax.sharding import PartitionSpec as P

EPSILON = 1e-06
HIGHEST = lax.Precision.HIGHEST
MESH = pl.DeviceIdType.MESH
TEAM = 4
F32 = jnp.float32
BF16 = jnp.bfloat16
VMEM = pl.BlockSpec(memory_space=pltpu.VMEM)
ANY = pl.BlockSpec(memory_space=pl.ANY)
CONTRACT_ROWS = (((0,), (0,)), ((), ()))
CONTRACT_COLS = (((1,), (1,)), ((), ()))


def place(n):
    sub = n // (TEAM * TEAM)
    me = lax.axis_index("fsdp")
    p = me // (TEAM * sub)
    t = lax.rem(me // sub, TEAM)
    s = lax.rem(me, sub)
    return sub, p, t, s, (lambda p, t, s: (p * (TEAM * sub) + t * sub + s,))


def greet(peers):
    barrier = pltpu.get_barrier_semaphore()
    for peer in peers:
        pl.semaphore_signal(barrier, inc=1, device_id=peer, device_id_type=MESH)
    pl.semaphore_wait(barrier, len(peers))


def remote(src, dst, send, recv, peer):
    return pltpu.make_async_remote_copy(
        src_ref=src, dst_ref=dst, send_sem=send, recv_sem=recv, device_id=peer, device_id_type=MESH
    )


def other(index, step, count):
    return lax.rem(index + step, count)


def spread_peers(sub, p, t, s, dev):
    peers = [dev(other(p, k, TEAM), t, s) for k in range(1, TEAM)]
    return peers + [dev(p, t, other(s, k, sub)) for k in range(1, sub)]


def team_peers(p, t, s, dev):
    return [dev(p, other(t, k, TEAM), s) for k in range(1, TEAM)]


def weights_start(n, w_ref, w_all, sems):
    sub, p, t, s, dev = place(n)
    p_send, p_recv, s_send, s_recv, own_sem = sems
    wide, near, local = [], [], []
    for i in range(w_ref.shape[0]):
        for k in range(1, TEAM):
            c = remote(w_ref.at[i], w_all.at[i, p, s], p_send.at[i, k], p_recv.at[i, k],
                       dev(other(p, k, TEAM), t, s))
            c.start()
            wide.append(c)
    for i in range(w_ref.shape[0]):
        for k in range(1, sub):
            c = remote(w_ref.at[i], w_all.at[i, p, s], s_send.at[i, 0, k], s_recv.at[i, 0, k],
                       dev(p, t, other(s, k, sub)))
            c.start()
            near.append(c)
        c = pltpu.make_async_copy(w_ref.at[i], w_all.at[i, p, s], own_sem.at[i])
        c.start()
        local.append(c)
    return wide, near, local


def weights_finish(n, w_all, sems, state):
    sub, p, t, s, dev = place(n)
    _, _, s_send, s_recv, _ = sems
    wide, near, local = state
    for i in range(w_all.shape[0]):
        for k in range(1, TEAM):
            wide[i * (TEAM - 1) + k - 1].wait_recv()
            q = other(p, TEAM - k, TEAM)
            for j in range(1, sub):
                c = remote(w_all.at[i, q, s], w_all.at[i, q, s], s_send.at[i, k, j], s_recv.at[i, k, j],
                           dev(p, t, other(s, j, sub)))
                c.start()
                near.append(c)
    for c in wide:
        c.wait_send()
    for c in near:
        c.wait()
    for c in local:
        c.wait()


def weights_sems(n, kinds):
    sub = n // (TEAM * TEAM)
    dma = pltpu.SemaphoreType.DMA
    return [dma((kinds, TEAM)), dma((kinds, TEAM)), dma((kinds, TEAM, sub)), dma((kinds, TEAM, sub)), dma((kinds,))]


def weights_shape(n, w):
    return jax.ShapeDtypeStruct((w.shape[0], TEAM, n // (TEAM * TEAM)) + w.shape[1:], w.dtype)


def gather_kernel(n, w_ref, tok_ref, dy_ref, meta_ref, w_all, tok_all, dy_all, meta_all,
                  t_send, t_recv, own_sem, *sems):
    sub, p, t, s, dev = place(n)
    greet(spread_peers(sub, p, t, s, dev) + team_peers(p, t, s, dev))
    state = weights_start(n, w_ref, w_all, sems)
    copies, local = [], []
    for i, (src, dst) in enumerate(((tok_ref, tok_all), (dy_ref, dy_all), (meta_ref, meta_all))):
        for k in range(1, TEAM):
            c = remote(src, dst.at[t], t_send.at[i, k], t_recv.at[i, k], dev(p, other(t, k, TEAM), s))
            c.start()
            copies.append(c)
        c = pltpu.make_async_copy(src, dst.at[t], own_sem.at[i])
        c.start()
        local.append(c)
    weights_finish(n, w_all, sems, state)
    for c in copies:
        c.wait()
    for c in local:
        c.wait()


def gather(n, w, tok, dy, meta):
    dma = pltpu.SemaphoreType.DMA
    shape = jax.ShapeDtypeStruct
    return pl.pallas_call(
        functools.partial(gather_kernel, n),
        out_shape=(
            weights_shape(n, w),
            shape((TEAM,) + tok.shape, BF16),
            shape((TEAM,) + dy.shape, BF16),
            shape((TEAM,) + meta.shape, jnp.int32),
        ),
        in_specs=[VMEM] * 4,
        out_specs=(ANY,) * 4,
        scratch_shapes=[dma((3, TEAM)), dma((3, TEAM)), dma((3,))] + weights_sems(n, w.shape[0]),
        compiler_params=pltpu.CompilerParams(collective_id=0, has_side_effects=True),
        name="gather_all",
    )(w, tok, dy, meta)


def middle_kernel(n, part_ref, x_ref, gain_ref, w_ref, y_ref, h_all, w_all, got, held,
                  a_send, a_recv, b_send, b_recv, own_sem, *sems):
    sub, p, t, s, dev = place(n)
    greet(spread_peers(sub, p, t, s, dev) + team_peers(p, t, s, dev))
    copies = []
    for k in range(1, TEAM):
        u = other(t, k, TEAM)
        c = remote(part_ref.at[u], got.at[k - 1], a_send.at[k], a_recv.at[k], dev(p, u, s))
        c.start()
        copies.append(c)
    state = weights_start(n, w_ref, w_all, sems)
    total = x_ref[...].astype(F32) + part_ref[t].astype(F32)
    for k in range(1, TEAM):
        copies[k - 1].wait_recv()
        total = total + got[k - 1].astype(F32)
    y_ref[...] = total
    scale = lax.rsqrt(jnp.mean(total * total, axis=-1, keepdims=True) + EPSILON)
    held[...] = (total * scale * gain_ref[1:2, :]).astype(BF16)
    local = pltpu.make_async_copy(held, h_all.at[t], own_sem)
    local.start()
    sends = []
    for k in range(1, TEAM):
        c = remote(held, h_all.at[t], b_send.at[k], b_recv.at[k], dev(p, other(t, k, TEAM), s))
        c.start()
        sends.append(c)
    weights_finish(n, w_all, sems, state)
    for c in copies:
        c.wait_send()
    for c in sends:
        c.wait()
    local.wait()


def middle_exchange(n, part, x, gains, w):
    dma = pltpu.SemaphoreType.DMA
    shape = jax.ShapeDtypeStruct
    return pl.pallas_call(
        functools.partial(middle_kernel, n),
        out_shape=(shape(x.shape, F32), shape((TEAM,) + x.shape, BF16), weights_shape(n, w)),
        in_specs=[VMEM] * 4,
        out_specs=(VMEM, ANY, ANY),
        scratch_shapes=[pltpu.VMEM((TEAM - 1,) + x.shape, BF16), pltpu.VMEM(x.shape, BF16),
                        dma((TEAM,)), dma((TEAM,)), dma((TEAM,)), dma((TEAM,)), dma] + weights_sems(n, w.shape[0]),
        compiler_params=pltpu.CompilerParams(collective_id=1, has_side_effects=True),
        name="middle_exchange",
    )(part, x, gains, w)


def reduce_kernel(n, m, h, *refs):
    parts, rows, grad_ref = refs[:m], refs[m:m + h], refs[m + h]
    refs = refs[m + h + 1:]
    outs, rows_all, grad_out = refs[:m], refs[m:m + h], refs[m + h]
    (got, sib, to_send, far, t_send, t_recv, h_send, h_recv, own_sem,
     s_send, s_recv, p_send, p_recv) = refs[m + h + 1:]
    sub, p, t, s, dev = place(n)
    greet(spread_peers(sub, p, t, s, dev) + team_peers(p, t, s, dev))
    kinds = grad_ref.shape[0]
    near, tokens, wide, shared, local = [], [], [], [], []
    for kind in range(kinds):
        for k in range(1, sub):
            v = other(s, k, sub)
            c = remote(grad_ref.at[kind, :, v], sib.at[kind, k - 1], s_send.at[kind, k], s_recv.at[kind, k],
                       dev(p, t, v))
            c.start()
            near.append(c)
    for i in range(h):
        for k in range(1, TEAM):
            c = remote(rows[i], rows_all[i].at[t], h_send.at[i, k], h_recv.at[i, k],
                       dev(p, other(t, k, TEAM), s))
            c.start()
            shared.append(c)
        c = pltpu.make_async_copy(rows[i], rows_all[i].at[t], own_sem.at[i])
        c.start()
        local.append(c)
    for i in range(m):
        for k in range(1, TEAM):
            u = other(t, k, TEAM)
            c = remote(parts[i].at[u], got.at[i, k - 1], t_send.at[i, k], t_recv.at[i, k], dev(p, u, s))
            c.start()
            tokens.append(c)
    for kind in range(kinds):
        for c in near[kind * (sub - 1):(kind + 1) * (sub - 1)]:
            c.wait_recv()
        for k in range(1, TEAM):
            q = other(p, k, TEAM)
            total = grad_ref[kind, q, s].astype(F32)
            for j in range(1, sub):
                total = total + sib[kind, j - 1, q].astype(F32)
            to_send[kind, k - 1] = total.astype(BF16)
            c = remote(to_send.at[kind, k - 1], far.at[kind, k - 1], p_send.at[kind, k], p_recv.at[kind, k],
                       dev(q, t, s))
            c.start()
            wide.append(c)
    for i in range(m):
        total = parts[i][t].astype(F32)
        for k in range(1, TEAM):
            tokens[i * (TEAM - 1) + k - 1].wait_recv()
            total = total + got[i, k - 1].astype(F32)
        outs[i][...] = total
    for kind in range(kinds):
        for c in wide[kind * (TEAM - 1):(kind + 1) * (TEAM - 1)]:
            c.wait_recv()
        total = grad_ref[kind, p, s].astype(F32)
        for j in range(1, sub):
            total = total + sib[kind, j - 1, p].astype(F32)
        for k in range(1, TEAM):
            total = total + far[kind, k - 1].astype(F32)
        grad_out[kind] = total
    for c in near + tokens + wide:
        c.wait_send()
    for c in shared:
        c.wait()
    for c in local:
        c.wait()


def reduce_exchange(n, parts, rows, grads, ident):
    sub = n // (TEAM * TEAM)
    m, h = len(parts), len(rows)
    dma = pltpu.SemaphoreType.DMA
    shape = jax.ShapeDtypeStruct
    block = parts[0].shape[1:] if m else (8, 128)
    kinds, tile = grads.shape[0], grads.shape[3:]
    outs = pl.pallas_call(
        functools.partial(reduce_kernel, n, m, h),
        out_shape=(shape(block, F32),) * m
        + tuple(shape((TEAM,) + v.shape, v.dtype) for v in rows)
        + (shape((kinds,) + tile, F32),),
        in_specs=[VMEM] * (m + h + 1),
        out_specs=(VMEM,) * m + (ANY,) * h + (VMEM,),
        scratch_shapes=[
            pltpu.VMEM((max(m, 1), TEAM - 1) + block, BF16),
            pltpu.VMEM((kinds, sub - 1, TEAM) + tile, BF16),
            pltpu.VMEM((kinds, TEAM - 1) + tile, BF16),
            pltpu.VMEM((kinds, TEAM - 1) + tile, BF16),
            dma((max(m, 1), TEAM)), dma((max(m, 1), TEAM)),
            dma((max(h, 1), TEAM)), dma((max(h, 1), TEAM)), dma((max(h, 1),)),
            dma((kinds, sub)), dma((kinds, sub)), dma((kinds, TEAM)), dma((kinds, TEAM)),
        ],
        compiler_params=pltpu.CompilerParams(collective_id=ident, has_side_effects=True),
        name=f"reduce_{ident}",
    )(*parts, *rows, grads)
    return outs[:m], outs[m:m + h], outs[m + h]


def small_kernel(n, x_ref, out_ref, got, mine, sib, held, far,
                 a_send, a_recv, s_send, s_recv, b_send, b_recv, c_send, c_recv):
    sub, p, t, s, dev = place(n)
    greet(spread_peers(sub, p, t, s, dev) + team_peers(p, t, s, dev))
    first, near, second, third = [], [], [], []
    for k in range(1, TEAM):
        u = other(t, k, TEAM)
        c = remote(x_ref.at[u], got.at[k - 1], a_send.at[k], a_recv.at[k], dev(p, u, s))
        c.start()
        first.append(c)
    total = x_ref[t]
    for k in range(1, TEAM):
        first[k - 1].wait_recv()
        total = total + got[k - 1]
    mine[...] = total
    sib[s] = total
    for k in range(1, sub):
        c = remote(mine, sib.at[s], s_send.at[k], s_recv.at[k], dev(p, t, other(s, k, sub)))
        c.start()
        near.append(c)
    for c in near:
        c.wait_recv()
    total = sib[0]
    for k in range(1, sub):
        total = total + sib[k]
    held[...] = total
    far[p] = total
    for k in range(1, TEAM):
        c = remote(held, far.at[p], b_send.at[k], b_recv.at[k], dev(other(p, k, TEAM), t, s))
        c.start()
        second.append(c)
    for c in second:
        c.wait_recv()
    total = far[0]
    for k in range(1, TEAM):
        total = total + far[k]
    out_ref[t] = total
    for k in range(1, TEAM):
        c = remote(out_ref.at[t], out_ref.at[t], c_send.at[k], c_recv.at[k], dev(p, other(t, k, TEAM), s))
        c.start()
        third.append(c)
    for c in first + near + second:
        c.wait_send()
    for c in third:
        c.wait()


def small_sum(n, x):
    sub = n // (TEAM * TEAM)
    dma = pltpu.SemaphoreType.DMA
    tile = x.shape[1:]
    return pl.pallas_call(
        functools.partial(small_kernel, n),
        out_shape=jax.ShapeDtypeStruct(x.shape, F32),
        in_specs=[VMEM],
        out_specs=VMEM,
        scratch_shapes=[pltpu.VMEM((TEAM - 1,) + tile, F32), pltpu.VMEM(tile, F32), pltpu.VMEM((sub,) + tile, F32),
                        pltpu.VMEM(tile, F32), pltpu.VMEM((TEAM,) + tile, F32)]
        + [dma((TEAM,)), dma((TEAM,)), dma((sub,)), dma((sub,))] + [dma((TEAM,))] * 4,
        compiler_params=pltpu.CompilerParams(collective_id=5, has_side_effects=True),
        name="small_sum",
    )(x)


def gelu_tanh(inner):
    return jax.nn.gelu(inner, approximate=True)


def norm_back(inputs, scale, gain, upstream):
    weighted = gain * upstream
    return scale * weighted - inputs * scale * scale * scale * jnp.mean(
        weighted * inputs, axis=-1, keepdims=True
    )


def dot_t(a, b):
    return lax.dot_general(a, b, CONTRACT_COLS, preferred_element_type=F32)


def dot_r(a, b):
    return lax.dot_general(a, b, CONTRACT_ROWS, preferred_element_type=F32)


def dot(a, b):
    return jnp.dot(a, b, preferred_element_type=F32)


def body(n, tokens, attn_weight, w_gate, w_up, w_down, norm_gains, bias_table, router,
         grad_out, segment, expert_ids, bucket_of):
    rows, width = tokens.shape
    slots = bucket_of.shape[0]
    routed = router.shape[1]
    buckets, head_count = bias_table.shape
    head_width = width // head_count
    factor = head_width ** (-0.5)
    heads = head_count // TEAM
    part = heads * head_width
    sub, _, t, _, _ = place(n)
    all_rows = TEAM * rows
    spans = all_rows // slots

    early = jnp.stack([attn_weight.T, w_down])
    late = jnp.stack([w_gate.T, w_up.T])
    meta = jnp.concatenate([segment[None], expert_ids.T, jnp.zeros((5, rows), jnp.int32)], axis=0)
    w_all, tok_all, dy_all, meta_all = gather(n, early, tokens, grad_out, meta)
    w_all = w_all.reshape(2, -1, width)
    attn_t, down = w_all[0], w_all[1]
    qkv_t, out_t = attn_t[: 3 * part], attn_t[3 * part :]
    inputs = tok_all.reshape(all_rows, width).astype(F32)
    segments = meta_all[:, 0, :].reshape(all_rows)
    id_a = meta_all[:, 1, :].reshape(all_rows)
    id_b = meta_all[:, 2, :].reshape(all_rows)

    places = jnp.arange(slots)
    gap = places[:, None] - places[None, :]
    causal = gap >= 0
    gap_hit = (gap[:, :, None] == places[None, None, :]).astype(F32)
    bucket_hit = (bucket_of[:, None] == jnp.arange(buckets)[None, :]).astype(F32)
    table_mine = lax.dynamic_slice(bias_table, (0, heads * t), (buckets, heads))
    by_gap = jnp.dot(bucket_hit, table_mine, precision=HIGHEST)
    offsets = jnp.einsum("ijd,dh->hij", gap_hit, by_gap, precision=HIGHEST)

    scale_one = lax.rsqrt(jnp.mean(inputs * inputs, axis=-1, keepdims=True) + EPSILON)
    normed = (inputs * scale_one * norm_gains[0]).astype(BF16)
    triple = dot_t(normed, qkv_t).astype(BF16)
    heads_of = lambda v: v.reshape(spans, slots, heads, head_width)
    query = heads_of(triple[:, :part])
    keyset = heads_of(triple[:, part : 2 * part])
    valueset = heads_of(triple[:, 2 * part :])
    seg = segments.reshape(spans, slots)
    allowed = (seg[:, :, None] == seg[:, None, :]) & causal[None]
    raw = jnp.einsum("bihd,bjhd->bhij", query, keyset, preferred_element_type=F32)
    scores = jnp.where(allowed[:, None], raw * factor + offsets[None], -1e30)
    peak = jnp.max(scores, axis=-1, keepdims=True)
    lifted_scores = jnp.exp(scores - peak)
    weights = lifted_scores / jnp.sum(lifted_scores, axis=-1, keepdims=True)
    weights_low = weights.astype(BF16)
    mixed = jnp.einsum("bhij,bjhd->bihd", weights_low, valueset, preferred_element_type=F32)
    mixed = mixed.reshape(all_rows, part).astype(BF16)
    branch = dot(mixed, out_t).astype(BF16).reshape(TEAM, rows, width)
    middle, second_all, late_all = middle_exchange(n, branch, tokens, norm_gains, late)
    late_all = late_all.reshape(2, -1, width)
    gate_t, up_t = late_all[0], late_all[1]
    second_all = second_all.reshape(all_rows, width)

    second_wide = second_all.astype(F32)
    probs_all = jax.nn.softmax(jnp.dot(second_wide, router, precision=HIGHEST), axis=-1)
    lanes = jnp.arange(routed)[None, :]
    picked_all = jnp.where((id_a[:, None] == lanes) | (id_b[:, None] == lanes), 1.0, 0.0)
    total_all = jnp.sum(probs_all * picked_all, axis=-1)
    live_all = picked_all[:, 0] * jnp.where(segments >= 0, 1.0, 0.0)
    combine_all = probs_all[:, 0] * live_all / total_all
    gated = dot_t(second_all, gate_t)
    lifted = dot_t(second_all, up_t)
    activated, gelu_back = jax.vjp(gelu_tanh, gated)
    hidden = (activated * lifted).astype(BF16)
    out_part = dot(hidden, down).astype(BF16).reshape(TEAM, rows, width)
    d_expert = (combine_all[:, None] * dy_all.reshape(all_rows, width).astype(F32)).astype(BF16)
    d_hidden = dot_t(d_expert, down)
    d_gated = gelu_back(d_hidden * lifted)[0].astype(BF16)
    d_lifted = (d_hidden * activated).astype(BF16)
    back_part = (dot(d_gated, gate_t) + dot(d_lifted, up_t)).astype(BF16).reshape(TEAM, rows, width)
    grad_ffn = jnp.stack(
        [dot_r(d_gated, second_all).astype(BF16), dot_r(d_lifted, second_all).astype(BF16)]
    ).reshape(2, TEAM, sub, -1, width)
    (expert_out, d_second), _, g_ffn = reduce_exchange(n, (out_part, back_part), (), grad_ffn, 2)
    grad_down = dot_r(hidden, d_expert).astype(BF16).reshape(1, TEAM, sub, -1, width)

    mine = lambda v: lax.dynamic_slice_in_dim(v, t * rows, rows, 0)
    second, probs, picked = mine(second_wide), mine(probs_all), mine(picked_all)
    chosen_total, live, combine = mine(total_all), mine(live_all), mine(combine_all)
    upstream = grad_out.astype(F32)
    result = (middle + combine[:, None] * expert_out).astype(BF16)
    d_combine = jnp.sum(expert_out * upstream, axis=-1)
    first_hot = jnp.where(jnp.arange(routed) == 0, 1.0, 0.0)
    ratio = probs[:, 0] / (chosen_total * chosen_total)
    d_probs = (d_combine * live)[:, None] * (
        first_hot[None, :] / chosen_total[:, None] - ratio[:, None] * picked
    )
    d_logits = probs * (d_probs - jnp.sum(d_probs * probs, axis=-1, keepdims=True))
    grad_router_t = lax.dot_general(d_logits, second, CONTRACT_ROWS, precision=HIGHEST)
    d_second = d_second + jnp.dot(d_logits, router.T, precision=HIGHEST)
    scale_two = lax.rsqrt(jnp.mean(middle * middle, axis=-1, keepdims=True) + EPSILON)
    gain_two = jnp.sum(d_second * middle * scale_two, axis=0)
    d_middle = upstream + norm_back(middle, scale_two, norm_gains[1], d_second)
    _, (d_branch,), g_down = reduce_exchange(n, (), (d_middle.astype(BF16),), grad_down, 3)
    d_branch = d_branch.reshape(all_rows, width)

    grad_out_t = dot_r(mixed, d_branch)
    d_mixed = heads_of(dot_t(d_branch, out_t).astype(BF16))
    d_weights = jnp.einsum("bihd,bjhd->bhij", d_mixed, valueset, preferred_element_type=F32)
    d_values = jnp.einsum("bhij,bihd->bjhd", weights_low, d_mixed, preferred_element_type=F32)
    d_scores = weights * (d_weights - jnp.sum(weights * d_weights, axis=-1, keepdims=True))
    d_scores = d_scores.astype(BF16)
    d_query = jnp.einsum("bhij,bjhd->bihd", d_scores, keyset, preferred_element_type=F32) * factor
    d_keys = jnp.einsum("bhij,bihd->bjhd", d_scores, query, preferred_element_type=F32) * factor
    score_sum = jnp.sum(d_scores.astype(F32), axis=0)
    gap_sum = jnp.einsum("hij,ijd->dh", score_sum, gap_hit, precision=HIGHEST)
    table_part = lax.dot_general(bucket_hit, gap_sum, CONTRACT_ROWS, precision=HIGHEST)
    grad_table = lax.dynamic_update_slice(jnp.zeros(bias_table.shape, F32), table_part, (0, heads * t))
    flat = lambda v: v.reshape(all_rows, part).astype(BF16)
    d_triple = jnp.concatenate([flat(d_query), flat(d_keys), flat(d_values)], axis=1)
    grad_in_t = dot_r(d_triple, normed)
    grad_attn = jnp.concatenate([grad_in_t, grad_out_t], axis=0).astype(BF16)
    grad_attn = grad_attn.reshape(1, TEAM, sub, -1, width)
    d_normed_part = dot(d_triple, qkv_t).astype(BF16).reshape(TEAM, rows, width)
    (d_normed,), _, g_attn = reduce_exchange(n, (d_normed_part,), (), grad_attn, 4)

    own_inputs = tokens.astype(F32)
    own_scale = mine(scale_one)
    gain_one = jnp.sum(d_normed * own_inputs * own_scale, axis=0)
    input_grad = (d_middle + norm_back(own_inputs, own_scale, norm_gains[0], d_normed)).astype(BF16)
    table_flat = grad_table.reshape(-1)
    lines = -(-table_flat.shape[0] // width)
    table_rows = jnp.pad(table_flat, (0, lines * width - table_flat.shape[0])).reshape(lines, width)
    small = jnp.concatenate([grad_router_t, gain_one[None], gain_two[None], table_rows], axis=0)
    depth = -(-small.shape[0] // (8 * TEAM)) * 8
    small = jnp.pad(small, ((0, depth * TEAM - small.shape[0]), (0, 0))).reshape(TEAM, depth, width)
    small = small_sum(n, small).reshape(TEAM * depth, width)
    grad_router = small[:routed].T
    grad_gains = small[routed : routed + 2]
    grad_table = small[routed + 2 : routed + 2 + lines].reshape(-1)[: table_flat.shape[0]].reshape(bias_table.shape)
    return (result, input_grad, g_attn[0].T, g_ffn[0].T, g_ffn[1].T, g_down[0],
            grad_gains, grad_table, grad_router)


def solution(mesh):
    n = mesh.shape["fsdp"]
    row, col = P("fsdp", None), P(None, "fsdp")
    in_specs = (row, col, col, col, row, P(), P(), P(), row, P("fsdp"), row, P())
    out_specs = (row, row, col, col, col, row, P(), P(), P())
    return jax.shard_map(
        functools.partial(body, n), mesh=mesh, in_specs=in_specs, out_specs=out_specs, check_vma=False
    )
```

time: 279 us -> 252 us (0.903)
  Pallas kernels: 194 us -> 167 us
    pallas_call x4, Pallas kernels: 142 us -> 110 us  [the longest x3 76.7 us: reduce_exchange(): pl.pallas_call(functools.partial(reduce_kernel, n, m, h), out_shape=(shap...]
    pallas_call x1, Pallas kernels: 24.2 us -> 32.2 us  [middle_exchange(): pl.pallas_call(functools.partial(middle_kernel, n), out_shape=(shape(x.sh...]
    slice x1 -> x2, local copies, waits for them, and re-layouts: 4.15 us -> 1.31 us  [the longest x1 1.16 us: body(): attn_t, down = (w_all[0], w_all[1])]
where the time goes in v2:
time: 252 us; the launch traced here: 251 us
  Pallas kernels  167 us (66%)
  matrix products  35.4 us (14%)
  local copies, waits for them, and re-layouts  24.3 us (10%)
  other arithmetic  22.1 us (9%)
    pallas_call x3, Pallas kernels, reduce_exchange(): pl.pallas_call(functools.partial(reduce_kernel, n, m, h), out_shape=(shap...  76.7 us
    pallas_call x1, Pallas kernels, gather(): pl.pallas_call(functools.partial(gather_kernel, n), out_shape=(weights_sh...  33.6 us
    pallas_call x1, Pallas kernels, middle_exchange(): pl.pallas_call(functools.partial(middle_kernel, n), out_shape=(shape(x.sh...  32.2 us
    pallas_call x1, Pallas kernels, small_sum(): pl.pallas_call(functools.partial(small_kernel, n), out_shape=jax.ShapeDty...  24.8 us
    dot_general x5, matrix products, dot(): return jnp.dot(a, b, preferred_element_type=F32)  7.19 us
    dot_general x5, matrix products, dot_t(): return lax.dot_general(a, b, CONTRACT_COLS, preferred_element_type=F32)  5.62 us
    dot_general x5, matrix products, dot_r(): return lax.dot_general(a, b, CONTRACT_ROWS, preferred_element_type=F32)  5.53 us
    unnamed x65, local copies, waits for them, and re-layouts  5.25 us

profile of v2, /device:TPU:0, one launch (start us, length us, event | category | flops | bytes accessed | tf_op | source)
XLA Modules:
  0.0 250.7 jit_solution(6610695285006756474)
XLA Ops:
  4.0 2.8 %fusion.2 = f32[3,64,64]{2,0,1:T(4,128)S(1)} fusion(f32[64,3,1]{0,1,2:T(4,128)S(1)} %convolution_bitcast_fusion, s32[64,64]{1,0:T(8,128)S(1)} %iota_subtract_fusion), kind=kOutput, calls=%fused_computation.6 | convolution fusion | flops 9699328 | bytes 66304 | tf_op jit(solution)/shard_map/ijd,dh->hij/dot_general | solution.py:414
  7.0 1.7 pad_maximum_fusion.2.w_ref
  9.4 33.6 %gather_all.1 = (bf16[2,4,2,96,768]{4,3,2,1,0:T(8,128)(2,1)}, bf16[4,128,768]{2,1,0:T(8,128)(2,1)}, bf16[4,128,768]{2,1,0:T(8,128)(2,1)}, s32[4,8,128]{2,1,0:T(8,128)}) custom-call(bf16[2,96,768]{2,1,0:T(8,128)(2,1)} %pad_maximum_fusion.2.w_ref, bf16[128,768]{1,0:T(8,128)(2,1)} %x_ref.1, bf16[128,768]{1,0:T(8,128)(2,1)} %dy_ref.1, s32[8,128]{1,0:T(8,128)} %add_add_fusion.meta_ref), custom_call_target="tpu_custom_call" | custom-call | tf_op jit(solution)/shard_map/gather_all/pallas_call | solution.py:133
  43.1 1.4 multiply_reduce_fusion
  54.7 2.1 fusion.19
  59.6 32.2 %middle_exchange.1 = (f32[128,768]{1,0:T(8,128)}, bf16[4,128,768]{2,1,0:T(8,128)(2,1)}, bf16[2,4,2,96,768]{4,3,2,1,0:T(8,128)(2,1)}) custom-call(bf16[4,128,768]{2,1,0:T(8,128)(2,1)} %bitcast.160, bf16[128,768]{1,0:T(8,128)(2,1)} %x_ref.1, f32[2,768]{1,0:T(2,128)} %gain_ref.1, bf16[2,96,768]{2,1,0:T(8,128)(2,1)} %pad_maximum_fusion.3.w_ref), custom_call_target="tpu_custom_call" | custom-call | tf_op jit(solution)/shard_map/middle_exchange/pallas_call | solution.py:185
  93.0 2.0 fusion.77
  96.0 1.5 fusion.11
  101.5 1.8 multiply_convert_fusion
  103.3 1.7 convolution_convert_fusion.4
  105.7 1.7 add_convert_fusion
  109.1 1.6 pad_maximum_fusion.refs_2_
  110.7 34.7 %reduce_2.1 = (f32[128,768]{1,0:T(8,128)}, f32[128,768]{1,0:T(8,128)}, f32[2,96,768]{2,1,0:T(8,128)}) custom-call(bf16[4,128,768]{2,1,0:T(8,128)(2,1)} %bitcast.187, bf16[4,128,768]{2,1,0:T(8,128)(2,1)} %bitcast.188, bf16[2,4,2,96,768]{4,3,2,1,0:T(8,128)(2,1)} %pad_maximum_fusion.refs_2_), custom_call_target="tpu_custom_call" | custom-call | tf_op jit(solution)/shard_map/reduce_2/pallas_call | solution.py:272
  149.4 1.8 multiply_reduce_fusion.2
  152.1 1.8 convolution_convert_fusion
  153.9 20.1 %reduce_3.1 = (bf16[4,128,768]{2,1,0:T(8,128)(2,1)}, f32[1,96,768]{2,1,0:T(8,128)}) custom-call(bf16[128,768]{1,0:T(8,128)(2,1)} %fusion.69.refs_0_, bf16[1,4,2,96,768]{4,3,2,1,0:T(8,128)(2,1)} %bitcast.171), custom_call_target="tpu_custom_call" | custom-call | tf_op jit(solution)/shard_map/reduce_3/pallas_call | solution.py:272
  174.0 1.5 convolution_convert_fusion.11
  175.6 1.5 convolution_convert_fusion.10
  178.0 2.6 %fusion.20 = bf16[8,64,3,64]{1,3,2,0:T(8,128)(2,1)} fusion(bf16[8,64,3,64]{1,0,3,2:T(8,128)(2,1)} %reshape.259, f32[8,3,64]{2,1,0:T(4,128)S(1)} %get-tuple-element.90, f32[8,3,64,64]{2,3,1,0:T(8,128)} %copy-done.15), kind=kOutput, calls=%fused_computation.47 | convolution fusion | flops 12977727 | bytes 792576 | tf_op jit(solution)/shard_map/bhij,bihd->bjhd/dot_general | solution.py:485
  189.6 1.7 convolution_convert_fusion.5
  193.1 21.9 %reduce_4.1 = (f32[128,768]{1,0:T(8,128)}, f32[1,96,768]{2,1,0:T(8,128)}) custom-call(bf16[4,128,768]{2,1,0:T(8,128)(2,1)} %bitcast.186, bf16[1,4,2,96,768]{4,3,2,1,0:T(8,128)(2,1)} %bitcast.157), custom_call_target="tpu_custom_call" | custom-call | tf_op jit(solution)/shard_map/reduce_4/pallas_call | solution.py:272
  216.2 2.1 fusion.32
  219.1 24.8 %small_sum.1 = f32[4,24,768]{2,1,0:T(8,128)} custom-call(f32[4,24,768]{2,1,0:T(8,128)} %bitcast.172), custom_call_target="tpu_custom_call" | custom-call | tf_op jit(solution)/shard_map/small_sum/pallas_call | solution.py:345
  246.0 1.6 slice_bitcast_fusion.2
  (148 shorter events, 48.8 us)
Async XLA Ops:
  0.6 92.3 %copy-start = (f32[768,64]{0,1:T(8,128)S(1)}, f32[768,64]{0,1:T(8,128)}, u32[]{:S(2)}) copy-start(f32[768,64]{0,1:T(8,128)} %param.19) | copy-start | bytes 589828
  0.7 8.0 %copy-start.25 = (bf16[768,96]{0,1:T(8,128)(2,1)S(1)}, bf16[768,96]{0,1:T(8,128)(2,1)}, u32[]{:S(2)}) copy-start(bf16[768,96]{0,1:T(8,128)(2,1)} %param.15) | copy-start | bytes 442372
  0.7 8.0 %copy-start.26 = (bf16[768,96]{0,1:T(8,128)(2,1)S(1)}, bf16[768,96]{0,1:T(8,128)(2,1)}, u32[]{:S(2)}) copy-start(bf16[768,96]{0,1:T(8,128)(2,1)} %param.14) | copy-start | bytes 442372
  43.1 4.2 %copy-start.1 = (bf16[4,128,768]{2,1,0:T(8,128)(2,1)S(1)}, bf16[4,128,768]{2,1,0:T(8,128)(2,1)}, u32[]{:S(2)}) copy-start(bf16[4,128,768]{2,1,0:T(8,128)(2,1)} %get-tuple-element.23) | copy-start | bytes 2359300
  47.3 1.9 copy-start.7
  49.3 1.8 copy-start.13
  53.2 1.5 copy-start.15
  59.6 36.4 %copy-start.4 = (bf16[4,128,768]{2,1,0:T(8,128)(2,1)S(1)}, bf16[4,128,768]{2,1,0:T(8,128)(2,1)}, u32[]{:S(2)}) copy-start(bf16[4,128,768]{2,1,0:T(8,128)(2,1)} %get-tuple-element.29) | copy-start | bytes 2359300
  96.0 2.2 copy-start.6
  103.3 1.7 copy-start.28
  110.7 34.7 %copy-start.5 = (bf16[128,768]{1,0:T(8,128)(2,1)S(1)}, bf16[128,768]{1,0:T(8,128)(2,1)}, u32[]{:S(2)}) copy-start(bf16[128,768]{1,0:T(8,128)(2,1)} %dy_ref.1) | copy-start | bytes 589828
  110.7 38.7 %copy-start.2 = (f32[128,768]{1,0:T(8,128)S(1)}, f32[128,768]{1,0:T(8,128)}, u32[]{:S(2)}) copy-start(f32[128,768]{1,0:T(8,128)} %get-tuple-element.26) | copy-start | bytes 1179652
  148.2 3.9 %copy-start.19 = (bf16[512,768]{1,0:T(8,128)(2,1)S(1)}, bf16[512,768]{1,0:T(8,128)(2,1)}, u32[]{:S(2)}) copy-start(bf16[512,768]{1,0:T(8,128)(2,1)} %get-tuple-element.98) | copy-start | bytes 2359300
  148.2 3.9 %copy-start.29 = (bf16[512,768]{1,0:T(8,128)(2,1)S(1)}, bf16[512,768]{1,0:T(8,128)(2,1)}, u32[]{:S(2)}) copy-start(bf16[512,768]{1,0:T(8,128)(2,1)} %copy-done.28) | copy-start | bytes 2359300
  186.2 2.6 %copy-start.27 = (s32[64]{0:T(128)S(1)}, s32[64]{0:T(128)}, u32[]{:S(2)}) copy-start(s32[64]{0:T(128)} %param.23) | copy-start | bytes 772
  186.5 3.1 %copy-start.16 = (bf16[512,192]{0,1:T(8,128)(2,1)S(1)}, bf16[512,192]{0,1:T(8,128)(2,1)}, u32[]{:S(2)}) copy-start(bf16[512,192]{0,1:T(8,128)(2,1)} %convert_element_type.186) | copy-start | bytes 589828
  186.8 2.9 %copy-start.14 = (bf16[1,3,2,96,768]{4,3,2,1,0:T(8,128)(2,1)S(1)}, bf16[1,3,2,96,768]{4,3,2,1,0:T(8,128)(2,1)}, u32[]{:S(2)}) copy-start(bf16[1,3,2,96,768]{4,3,2,1,0:T(8,128)(2,1)} %copy-done.13) | copy-start | bytes 2654212
  187.7 1.8 copy-start.17
  189.6 1.8 copy-start.18
  193.1 21.9 %copy-start.3 = (bf16[128,768]{1,0:T(8,128)(2,1)S(1)}, bf16[128,768]{1,0:T(8,128)(2,1)}, u32[]{:S(2)}) copy-start(bf16[128,768]{1,0:T(8,128)(2,1)} %x_ref.1) | copy-start | bytes 589828
  193.1 23.1 %copy-start.10 = (f32[128,768]{1,0:T(8,128)S(1)}, f32[128,768]{1,0:T(8,128)}, u32[]{:S(2)}) copy-start(f32[128,768]{1,0:T(8,128)} %get-tuple-element.30) | copy-start | bytes 1179652
  216.2 32.2 %copy-start.20 = (f32[2,96,768]{2,1,0:T(8,128)S(1)}, f32[2,96,768]{2,1,0:T(8,128)}, u32[]{:S(2)}) copy-start(f32[2,96,768]{2,1,0:T(8,128)} %get-tuple-element.35) | copy-start | bytes 1769476
  218.3 30.9 %copy-start.24 = (f32[1,96,768]{2,1,0:T(8,128)S(1)}, f32[1,96,768]{2,1,0:T(8,128)}, u32[]{:S(2)}) copy-start(f32[1,96,768]{2,1,0:T(8,128)} %get-tuple-element.34) | copy-start | bytes 884740
  218.3 31.6 %copy-start.23 = (f32[1,96,768]{2,1,0:T(8,128)S(1)}, f32[1,96,768]{2,1,0:T(8,128)}, u32[]{:S(2)}) copy-start(f32[1,96,768]{2,1,0:T(8,128)} %get-tuple-element.36) | copy-start | bytes 884740
  (6 other events, 6.3 us)

commit v3 on v2

--- a/solution.py
+++ b/solution.py
@@ -194,12 +194,20 @@
     )(part, x, gains, w)
 
 
-def reduce_kernel(n, m, h, *refs):
+def reduce_kernel(n, m, h, gain_row, *refs):
     parts, rows, grad_ref = refs[:m], refs[m:m + h], refs[m + h]
     refs = refs[m + h + 1:]
+    small = gain_row is not None
+    if small:
+        unit_ref, small_ref = refs[:2]
+        refs = refs[2:]
     outs, rows_all, grad_out = refs[:m], refs[m:m + h], refs[m + h]
+    if small:
+        small_out = refs[m + h + 1]
+        refs = refs[:m + h + 1] + refs[m + h + 2:]
     (got, sib, to_send, far, t_send, t_recv, h_send, h_recv, own_sem,
-     s_send, s_recv, p_send, p_recv) = refs[m + h + 1:]
+     s_send, s_recv, p_send, p_recv) = refs[m + h + 1:m + h + 14]
+    rest = refs[m + h + 14:]
     sub, p, t, s, dev = place(n)
     greet(spread_peers(sub, p, t, s, dev) + team_peers(p, t, s, dev))
     kinds = grad_ref.shape[0]
@@ -245,6 +253,13 @@
             tokens[i * (TEAM - 1) + k - 1].wait_recv()
             total = total + got[i, k - 1].astype(F32)
         outs[i][...] = total
+    if small:
+        buf = rest[0]
+        piece, line = divmod(gain_row, small_ref.shape[1])
+        gain = jnp.sum(outs[0][...] * unit_ref[...], axis=0, keepdims=True)
+        buf[...] = small_ref[...]
+        buf[piece, line:line + 1, :] = gain
+        small_phases(n, buf, small_out, *rest[1:])
     for kind in range(kinds):
         for c in wide[kind * (TEAM - 1):(kind + 1) * (TEAM - 1)]:
             c.wait_recv()
@@ -262,7 +277,7 @@
         c.wait()
 
 
-def reduce_exchange(n, parts, rows, grads, ident):
+def reduce_exchange(n, parts, rows, grads, ident, small=(), gain_row=None):
     sub = n // (TEAM * TEAM)
     m, h = len(parts), len(rows)
     dma = pltpu.SemaphoreType.DMA
@@ -270,12 +285,13 @@
     block = parts[0].shape[1:] if m else (8, 128)
     kinds, tile = grads.shape[0], grads.shape[3:]
     outs = pl.pallas_call(
-        functools.partial(reduce_kernel, n, m, h),
+        functools.partial(reduce_kernel, n, m, h, gain_row),
         out_shape=(shape(block, F32),) * m
         + tuple(shape((TEAM,) + v.shape, v.dtype) for v in rows)
-        + (shape((kinds,) + tile, F32),),
-        in_specs=[VMEM] * (m + h + 1),
-        out_specs=(VMEM,) * m + (ANY,) * h + (VMEM,),
+        + (shape((kinds,) + tile, F32),)
+        + tuple(shape(v.shape, F32) for v in small[1:]),
+        in_specs=[VMEM] * (m + h + 1 + len(small)),
+        out_specs=(VMEM,) * m + (ANY,) * h + (VMEM,) * (1 + len(small[1:])),
         scratch_shapes=[
             pltpu.VMEM((max(m, 1), TEAM - 1) + block, BF16),
             pltpu.VMEM((kinds, sub - 1, TEAM) + tile, BF16),
@@ -284,24 +300,23 @@
             dma((max(m, 1), TEAM)), dma((max(m, 1), TEAM)),
             dma((max(h, 1), TEAM)), dma((max(h, 1), TEAM)), dma((max(h, 1),)),
             dma((kinds, sub)), dma((kinds, sub)), dma((kinds, TEAM)), dma((kinds, TEAM)),
-        ],
+        ] + (small_scratch(n, small[1].shape) if small else []),
         compiler_params=pltpu.CompilerParams(collective_id=ident, has_side_effects=True),
         name=f"reduce_{ident}",
-    )(*parts, *rows, grads)
-    return outs[:m], outs[m:m + h], outs[m + h]
-
-
-def small_kernel(n, x_ref, out_ref, got, mine, sib, held, far,
+    )(*parts, *rows, grads, *small)
+    return (outs[:m], outs[m:m + h]) + tuple(outs[m + h:])
+
+
+def small_phases(n, buf, out_ref, got, mine, sib, held, far,
                  a_send, a_recv, s_send, s_recv, b_send, b_recv, c_send, c_recv):
     sub, p, t, s, dev = place(n)
-    greet(spread_peers(sub, p, t, s, dev) + team_peers(p, t, s, dev))
     first, near, second, third = [], [], [], []
     for k in range(1, TEAM):
         u = other(t, k, TEAM)
-        c = remote(x_ref.at[u], got.at[k - 1], a_send.at[k], a_recv.at[k], dev(p, u, s))
+        c = remote(buf.at[u], got.at[k - 1], a_send.at[k], a_recv.at[k], dev(p, u, s))
         c.start()
         first.append(c)
-    total = x_ref[t]
+    total = buf[t]
     for k in range(1, TEAM):
         first[k - 1].wait_recv()
         total = total + got[k - 1]
@@ -338,21 +353,13 @@
         c.wait()
 
 
-def small_sum(n, x):
+def small_scratch(n, shape):
     sub = n // (TEAM * TEAM)
     dma = pltpu.SemaphoreType.DMA
-    tile = x.shape[1:]
-    return pl.pallas_call(
-        functools.partial(small_kernel, n),
-        out_shape=jax.ShapeDtypeStruct(x.shape, F32),
-        in_specs=[VMEM],
-        out_specs=VMEM,
-        scratch_shapes=[pltpu.VMEM((TEAM - 1,) + tile, F32), pltpu.VMEM(tile, F32), pltpu.VMEM((sub,) + tile, F32),
-                        pltpu.VMEM(tile, F32), pltpu.VMEM((TEAM,) + tile, F32)]
-        + [dma((TEAM,)), dma((TEAM,)), dma((sub,)), dma((sub,))] + [dma((TEAM,))] * 4,
-        compiler_params=pltpu.CompilerParams(collective_id=5, has_side_effects=True),
-        name="small_sum",
-    )(x)
+    tile = shape[1:]
+    return [pltpu.VMEM(shape, F32), pltpu.VMEM((TEAM - 1,) + tile, F32), pltpu.VMEM(tile, F32),
+            pltpu.VMEM((sub,) + tile, F32), pltpu.VMEM(tile, F32), pltpu.VMEM((TEAM,) + tile, F32),
+            dma((TEAM,)), dma((TEAM,)), dma((sub,)), dma((sub,))] + [dma((TEAM,))] * 4
 
 
 def gelu_tanh(inner):
@@ -497,19 +504,19 @@
     grad_attn = jnp.concatenate([grad_in_t, grad_out_t], axis=0).astype(BF16)
     grad_attn = grad_attn.reshape(1, TEAM, sub, -1, width)
     d_normed_part = dot(d_triple, qkv_t).astype(BF16).reshape(TEAM, rows, width)
-    (d_normed,), _, g_attn = reduce_exchange(n, (d_normed_part,), (), grad_attn, 4)
-
     own_inputs = tokens.astype(F32)
     own_scale = mine(scale_one)
-    gain_one = jnp.sum(d_normed * own_inputs * own_scale, axis=0)
-    input_grad = (d_middle + norm_back(own_inputs, own_scale, norm_gains[0], d_normed)).astype(BF16)
     table_flat = grad_table.reshape(-1)
     lines = -(-table_flat.shape[0] // width)
     table_rows = jnp.pad(table_flat, (0, lines * width - table_flat.shape[0])).reshape(lines, width)
-    small = jnp.concatenate([grad_router_t, gain_one[None], gain_two[None], table_rows], axis=0)
+    small = jnp.concatenate([grad_router_t, jnp.zeros((1, width), F32), gain_two[None], table_rows], axis=0)
     depth = -(-small.shape[0] // (8 * TEAM)) * 8
     small = jnp.pad(small, ((0, depth * TEAM - small.shape[0]), (0, 0))).reshape(TEAM, depth, width)
-    small = small_sum(n, small).reshape(TEAM * depth, width)
+    (d_normed,), _, g_attn, small = reduce_exchange(
+        n, (d_normed_part,), (), grad_attn, 4, (own_inputs * own_scale, small), routed
+    )
+    small = small.reshape(TEAM * depth, width)
+    input_grad = (d_middle + norm_back(own_inputs, own_scale, norm_gains[0], d_normed)).astype(BF16)
     grad_router = small[:routed].T
     grad_gains = small[routed : routed + 2]
     grad_table = small[routed + 2 : routed + 2 + lines].reshape(-1)[: table_flat.shape[0]].reshape(bias_table.shape)

time: 252 us -> 238 us (0.944)
  Pallas kernels: 167 us -> 158 us
  matrix products: 35.4 us -> 32.8 us
    pallas_call x4 -> x3, Pallas kernels: 102 us -> 91.9 us  [reduce_exchange(): pl.pallas_call(functools.partial(reduce_kernel, n, m, h, gain_row), out_s...]
    unnamed x65 -> x117, local copies, waits for them, and re-layouts: 5.25 us -> 5.73 us
where the time goes in v3:
time: 238 us; the launch traced here: 237 us
  Pallas kernels  158 us (66%)
  matrix products  32.8 us (14%)
  other arithmetic  22.9 us (10%)
  local copies, waits for them, and re-layouts  21.9 us (9%)
    pallas_call x3, Pallas kernels, reduce_exchange(): pl.pallas_call(functools.partial(reduce_kernel, n, m, h, gain_row), out_s...  91.9 us
    pallas_call x1, Pallas kernels, gather(): pl.pallas_call(functools.partial(gather_kernel, n), out_shape=(weights_sh...  33.6 us
    pallas_call x1, Pallas kernels, middle_exchange(): pl.pallas_call(functools.partial(middle_kernel, n), out_shape=(shape(x.sh...  32.2 us
    dot_general x5, matrix products, dot(): return jnp.dot(a, b, preferred_element_type=F32)  8.42 us
    unnamed x117, local copies, waits for them, and re-layouts  5.73 us
    dot_general x5, matrix products, dot_t(): return lax.dot_general(a, b, CONTRACT_COLS, preferred_element_type=F32)  5.64 us

profile of v3, /device:TPU:0, one launch (start us, length us, event | category | flops | bytes accessed | tf_op | source)
XLA Modules:
  0.0 236.8 jit_solution(1110132161735008140)
XLA Ops:
  1.7 2.8 %fusion.2 = f32[3,64,64]{2,0,1:T(4,128)S(1)} fusion(f32[64,3,1]{0,1,2:T(4,128)S(1)} %convolution_bitcast_fusion, s32[64,64]{1,0:T(8,128)S(1)} %iota_subtract_fusion), kind=kOutput, calls=%fused_computation.6 | convolution fusion | flops 9699328 | bytes 66304 | tf_op jit(solution)/shard_map/ijd,dh->hij/dot_general | solution.py:421
  4.6 1.7 pad_maximum_fusion.2.w_ref
  7.1 33.6 %gather_all.1 = (bf16[2,4,2,96,768]{4,3,2,1,0:T(8,128)(2,1)}, bf16[4,128,768]{2,1,0:T(8,128)(2,1)}, bf16[4,128,768]{2,1,0:T(8,128)(2,1)}, s32[4,8,128]{2,1,0:T(8,128)}) custom-call(bf16[2,96,768]{2,1,0:T(8,128)(2,1)} %pad_maximum_fusion.2.w_ref, bf16[128,768]{1,0:T(8,128)(2,1)} %x_ref.1, bf16[128,768]{1,0:T(8,128)(2,1)} %dy_ref.1, s32[8,128]{1,0:T(8,128)} %add_add_fusion.meta_ref), custom_call_target="tpu_custom_call" | custom-call | tf_op jit(solution)/shard_map/gather_all/pallas_call | solution.py:133
  40.8 1.4 fusion.66
  42.5 1.4 multiply_reduce_fusion
  44.5 1.4 multiply_convert_fusion.3
  50.1 1.4 fusion.68
  54.4 1.4 convolution_convert_fusion.6
  56.5 32.2 %middle_exchange.1 = (f32[128,768]{1,0:T(8,128)}, bf16[4,128,768]{2,1,0:T(8,128)(2,1)}, bf16[2,4,2,96,768]{4,3,2,1,0:T(8,128)(2,1)}) custom-call(bf16[4,128,768]{2,1,0:T(8,128)(2,1)} %bitcast.161, bf16[128,768]{1,0:T(8,128)(2,1)} %x_ref.1, f32[2,768]{1,0:T(2,128)} %gain_ref.1, bf16[2,96,768]{2,1,0:T(8,128)(2,1)} %pad_maximum_fusion.3.w_ref), custom_call_target="tpu_custom_call" | custom-call | tf_op jit(solution)/shard_map/middle_exchange/pallas_call | solution.py:185
  89.8 1.9 fusion.63
  95.4 1.8 multiply_convert_fusion
  97.3 1.7 convolution_convert_fusion.4
  99.7 1.7 add_convert_fusion
  103.1 1.6 pad_maximum_fusion.refs_2_
  104.7 34.7 %reduce_2.1 = (f32[128,768]{1,0:T(8,128)}, f32[128,768]{1,0:T(8,128)}, f32[2,96,768]{2,1,0:T(8,128)}) custom-call(bf16[4,128,768]{2,1,0:T(8,128)(2,1)} %bitcast.185, bf16[4,128,768]{2,1,0:T(8,128)(2,1)} %bitcast.186, bf16[2,4,2,96,768]{4,3,2,1,0:T(8,128)(2,1)} %pad_maximum_fusion.refs_2_), custom_call_target="tpu_custom_call" | custom-call | tf_op jit(solution)/shard_map/reduce_2/pallas_call | solution.py:287
  142.2 1.7 multiply_reduce_fusion.2
  146.1 2.1 convolution_convert_fusion
  148.2 20.2 %reduce_3.1 = (bf16[4,128,768]{2,1,0:T(8,128)(2,1)}, f32[1,96,768]{2,1,0:T(8,128)}) custom-call(bf16[128,768]{1,0:T(8,128)(2,1)} %fusion.61.refs_0_, bf16[1,4,2,96,768]{4,3,2,1,0:T(8,128)(2,1)} %bitcast.172), custom_call_target="tpu_custom_call" | custom-call | tf_op jit(solution)/shard_map/reduce_3/pallas_call | solution.py:287
  168.4 1.5 convolution_convert_fusion.11
  176.4 2.5 %fusion.20 = bf16[8,64,3,64]{1,3,2,0:T(8,128)(2,1)} fusion(bf16[8,64,3,64]{1,0,3,2:T(8,128)(2,1)S(1)} %copy-done.22, f32[8,3,64]{2,1,0:T(4,128)S(1)} %copy-done.29, f32[8,3,64,64]{2,3,1,0:T(8,128)} %copy-done.16), kind=kOutput, calls=%fused_computation.47 | convolution fusion | flops 12977727 | bytes 792576 | tf_op jit(solution)/shard_map/bhij,bihd->bjhd/dot_general | solution.py:492
  178.9 1.3 copy.78
  181.2 2.9 %convolution_convert_fusion.5 = bf16[512,768]{1,0:T(8,128)(2,1)} fusion(bf16[512,576]{0,1:T(8,128)(2,1)} %constant_dynamic-update-slice_fusion, bf16[576,768]{1,0:T(8,128)(2,1)S(1)} %bitcast.181), kind=kOutput, calls=%fused_computation.32 | convolution fusion | flops 453378048 | bytes 2260992 | tf_op jit(solution)/shard_map/dot_general | solution.py:385
  191.3 37.0 %reduce_4.1 = (f32[128,768]{1,0:T(8,128)}, f32[1,96,768]{2,1,0:T(8,128)}, f32[4,24,768]{2,1,0:T(8,128)}) custom-call(bf16[4,128,768]{2,1,0:T(8,128)(2,1)} %bitcast.184, bf16[1,4,2,96,768]{4,3,2,1,0:T(8,128)(2,1)} %bitcast.158, f32[128,768]{1,0:T(8,128)} %convert_multiply_fusion.1.refs_2_, f32[4,24,768]{2,1,0:T(8,128)} %bitcast.173), custom_call_target="tpu_custom_call" | custom-call | tf_op jit(solution)/shard_map/reduce_4/pallas_call | solution.py:287
  230.3 2.1 add_convert_fusion.1
  (201 shorter events, 43.1 us)
Async XLA Ops:
  0.6 92.7 %copy-start = (f32[768,64]{0,1:T(8,128)S(1)}, f32[768,64]{0,1:T(8,128)}, u32[]{:S(2)}) copy-start(f32[768,64]{0,1:T(8,128)} %param.19) | copy-start | bytes 589828
  0.7 5.8 %copy-start.51 = (s32[128,2]{0,1:T(2,128)S(1)}, s32[128,2]{0,1:T(2,128)}, u32[]{:S(2)}) copy-start(s32[128,2]{0,1:T(2,128)} %param.22) | copy-start | bytes 3076
  0.7 5.8 %copy-start.52 = (s32[128]{0:T(128)S(1)}, s32[128]{0:T(128)}, u32[]{:S(2)}) copy-start(s32[128]{0:T(128)} %param.21) | copy-start | bytes 1540
  0.7 41.8 %copy-start.33 = (f32[2,768]{1,0:T(2,128)S(1)}, f32[2,768]{1,0:T(2,128)}, u32[]{:S(2)}) copy-start(f32[2,768]{1,0:T(2,128)} %gain_ref.1) | copy-start | bytes 18436
  1.7 44.2 %copy-start.31 = (s32[64,64]{1,0:T(8,128)}, s32[64,64]{1,0:T(8,128)S(1)}, u32[]{:S(2)}) copy-start(s32[64,64]{1,0:T(8,128)S(1)} %iota_subtract_fusion) | copy-start | bytes 49156
  89.8 54.1 %copy-start.43 = (f32[128]{0:T(128)}, f32[128]{0:T(128)S(1)}, u32[]{:S(2)}) copy-start(f32[128]{0:T(128)S(1)} %add_rsqrt_fusion.1) | copy-start | bytes 1540
  104.7 34.7 %copy-start.6 = (bf16[128,768]{1,0:T(8,128)(2,1)S(1)}, bf16[128,768]{1,0:T(8,128)(2,1)}, u32[]{:S(2)}) copy-start(bf16[128,768]{1,0:T(8,128)(2,1)} %dy_ref.1) | copy-start | bytes 589828
  104.7 37.5 %copy-start.2 = (f32[128,768]{1,0:T(8,128)S(1)}, f32[128,768]{1,0:T(8,128)}, u32[]{:S(2)}) copy-start(f32[128,768]{1,0:T(8,128)} %get-tuple-element.27) | copy-start | bytes 1179652
  139.4 5.4 %copy-start.1 = (bf16[4,128,768]{2,1,0:T(8,128)(2,1)S(1)}, bf16[4,128,768]{2,1,0:T(8,128)(2,1)}, u32[]{:S(2)}) copy-start(bf16[4,128,768]{2,1,0:T(8,128)(2,1)} %get-tuple-element.24) | copy-start | bytes 2359300
  139.5 5.4 %copy-start.34 = (f32[512]{0:T(512)S(1)}, f32[512]{0:T(512)}, u32[]{:S(2)}) copy-start(f32[512]{0:T(512)} %get-tuple-element.86) | copy-start | bytes 6148
  142.0 4.0 %copy-start.37 = (f32[128]{0:T(128)}, f32[128]{0:T(128)S(1)}, u32[]{:S(2)}) copy-start(f32[128]{0:T(128)S(1)} %get-tuple-element.88) | copy-start | bytes 1540
  142.0 4.0 %copy-start.39 = (f32[128]{0:T(128)}, f32[128]{0:T(128)S(1)}, u32[]{:S(2)}) copy-start(f32[128]{0:T(128)S(1)} %get-tuple-element.89) | copy-start | bytes 1540
  142.0 4.0 %copy-start.41 = (f32[128]{0:T(128)}, f32[128]{0:T(128)S(1)}, u32[]{:S(2)}) copy-start(f32[128]{0:T(128)S(1)} %get-tuple-element.99) | copy-start | bytes 1540
  142.1 4.0 %copy-start.45 = (f32[64]{0:T(128)}, f32[64]{0:T(128)S(1)}, u32[]{:S(2)}) copy-start(f32[64]{0:T(128)S(1)} %compare_select_fusion.1) | copy-start | bytes 772
  142.2 3.9 %copy-start.47 = (f32[128]{0:T(128)}, f32[128]{0:T(128)S(1)}, u32[]{:S(2)}) copy-start(f32[128]{0:T(128)S(1)} %multiply_reduce_fusion.6) | copy-start | bytes 1540
  148.2 22.8 %copy-start.21 = (bf16[8,64,3,64]{3,1,2,0:T(8,128)(2,1)S(1)}, bf16[8,64,3,64]{3,1,2,0:T(8,128)(2,1)}, u32[]{:S(2)}) copy-start(bf16[8,64,3,64]{3,1,2,0:T(8,128)(2,1)} %copy-done.20) | copy-start | bytes 589828
  148.2 22.8 %copy-start.29 = (f32[8,3,64]{2,1,0:T(4,128)S(1)}, f32[8,3,64]{2,1,0:T(4,128)}, u32[]{:S(2)}) copy-start(f32[8,3,64]{2,1,0:T(4,128)} %copy-done.28) | copy-start | bytes 18436
  185.2 3.9 %copy-start.38 = (f32[128]{0:T(128)S(1)}, f32[128]{0:T(128)}, u32[]{:S(2)}) copy-start(f32[128]{0:T(128)} %copy-done.37) | copy-start | bytes 1540
  185.2 3.9 %copy-start.40 = (f32[128]{0:T(128)S(1)}, f32[128]{0:T(128)}, u32[]{:S(2)}) copy-start(f32[128]{0:T(128)} %copy-done.39) | copy-start | bytes 1540
  191.3 39.0 %copy-start.12 = (f32[128,768]{1,0:T(8,128)S(1)}, f32[128,768]{1,0:T(8,128)}, u32[]{:S(2)}) copy-start(f32[128,768]{1,0:T(8,128)} %get-tuple-element.31) | copy-start | bytes 1179652
  191.3 39.0 %copy-start.44 = (f32[128]{0:T(128)S(1)}, f32[128]{0:T(128)}, u32[]{:S(2)}) copy-start(f32[128]{0:T(128)} %copy-done.43) | copy-start | bytes 1540
  191.3 39.0 %copy-start.50 = (f32[128]{0:T(128)S(1)}, f32[128]{0:T(128)}, u32[]{:S(2)}) copy-start(f32[128]{0:T(128)} %copy-done.49) | copy-start | bytes 1540
  228.3 4.1 %copy-start.18 = (f32[2,96,768]{2,1,0:T(8,128)S(1)}, f32[2,96,768]{2,1,0:T(8,128)}, u32[]{:S(2)}) copy-start(f32[2,96,768]{2,1,0:T(8,128)} %get-tuple-element.36) | copy-start | bytes 1769476
  230.2 5.1 %copy-start.24 = (f32[1,96,768]{2,1,0:T(8,128)S(1)}, f32[1,96,768]{2,1,0:T(8,128)}, u32[]{:S(2)}) copy-start(f32[1,96,768]{2,1,0:T(8,128)} %get-tuple-element.35) | copy-start | bytes 884740
  (32 other events, 69.1 us)
